TPU v7x, 256 devices: a whole 4x4x8 slice. The times are simulated.
256 devices in a mesh: bead: 32 (over y, z), space: 8 (over x, core).
Axes of the slice: x: 4, y: 4, z: 8, core: 2. Of those that a mesh axis runs over, the one named last changes fastest.
Arguments:
- positions: float32 [32, 3, 131072], P('bead', None, 'space'), may hold values from -5.5 to 5.5
- charges: float32 [131072], P('space'), may hold values from -1 to 1
- polarizability: float32 [131072], P('space'), may hold values from 0.03 to 0.12
- masses: float32 [131072], P('space'), may hold values from 1 to 16
- neighbors: int32 [1024, 8], P('space'), may hold values from 0 to 135, as said below
Outputs:
- forces: float32 [32, 3, 131072], P('bead', None, 'space')
- dipoles: float32 [3, 131072], P(None, ('space', 'bead'))
Inputs may be any that keep to these rules, and one draw needn't show every extreme that they name: `neighbors`: row t lists 8 different tiles by their index in its domain's extended numbering: the last 4 tiles of the previous domain, the domain's own 128 tiles, the first 4 tiles of the next domain (domains form a cycle). Every listed tile lies within 4 tiles of tile t, and the two tiles at distance exactly 4 on either side are always listed.
All inputs are finite; a program needn't handle non-finite values.
Results may differ from a plain program's by a relative error of at most 0.0001.
Values sent between devices are 32-bit elements; how exact they have to be, the bound alone decides.
No kernel may reach another device: no remote copies, remote signals or barrier semaphores. Data moves between devices by JAX's collectives and lax.ppermute only.
A program may use at most 64 MiB of HBM per device.

v0:
```python
import math

import jax
import jax.numpy as jnp
from jax import lax
from jax.sharding import PartitionSpec as P

TILE = 128
HALO_T = 4
ITERS = 3


REPULSION = 0.2
SPRING = 0.1


def extended_2(value, sides, width):
    for axis, dim in sides:
        size, length = (lax.axis_size(axis), value.shape[dim])
        up = [(i, (i + 1) % size) for i in range(size)]
        down = [(j, i) for i, j in up]
        last = lax.slice_in_dim(value, length - width, length, axis=dim)
        first = lax.slice_in_dim(value, 0, width, axis=dim)
        before = lax.ppermute(last, axis, up)
        after = lax.ppermute(first, axis, down)
        value = jnp.concatenate([before, value, after], axis=dim)
    return value


def repulsion_kernel(targets, sources):
    displace = targets[:, :, :, None] - sources[:, :, None, :]
    weight = jnp.exp(-0.5 * jnp.sum(displace * displace, axis=0))
    return REPULSION * jnp.sum(weight[None] * displace, axis=3)


def charge_kernel(targets, sources, charge):
    displace = targets[:, :, :, None] - sources[:, :, None, :]
    weight = jnp.exp(-0.25 * jnp.sum(displace * displace, axis=0)) * charge[0][:, None, :]
    return jnp.sum(weight[None] * displace, axis=3)


def dipole_kernel(targets, sources, dipole):
    displace = targets[:, :, :, None] - sources[:, :, None, :]
    weight = jnp.exp(-0.25 * jnp.sum(displace * displace, axis=0))
    spread_dip = dipole[:, :, None, :]
    projected = jnp.sum(displace * spread_dip, axis=0)
    return jnp.sum(weight[None] * (0.25 * displace * projected[None] - 0.5 * spread_dip), axis=3)


def grouped(kernel, targets, sources):
    tile_count = targets.shape[1]
    group_size = math.gcd(tile_count, 4)

    def split_tiles(tensor):
        return jnp.moveaxis(
            tensor.reshape(tensor.shape[0], tile_count // group_size, group_size, tensor.shape[2]),
            1,
            0,
        )

    pieces = tuple((split_tiles(tensor) for tensor in (targets,) + tuple(sources)))
    result = lax.map(lambda member: kernel(*member), pieces)
    return jnp.moveaxis(result, 0, 1).reshape(3, tile_count, targets.shape[2])


def gather_local(extended, tile_rows):
    channels = extended.shape[0]
    tiles = extended.reshape(channels, extended.shape[1] // TILE, TILE)
    picked = jnp.take(tiles, tile_rows, axis=1)
    return picked.reshape(channels, tile_rows.shape[0], tile_rows.shape[1] * TILE)


def per_device(positions, charges, polarizability, masses, neighbors):
    coords = positions[0]
    atom_dev = coords.shape[1]
    rim_width = HALO_T * TILE
    tiles_domain = atom_dev // TILE
    beads = lax.axis_size("bead")
    bead_index = lax.axis_index("bead")
    own_tiles = tiles_domain // beads
    own_start = bead_index * own_tiles
    cycle_rows = extended_2(positions, (("bead", 0),), 1)
    spring = SPRING * masses[None, :] * (cycle_rows[0] + cycle_rows[2] - 2.0 * coords)
    extended = extended_2(coords, (("space", 1),), rim_width)
    targets = coords.reshape(3, tiles_domain, TILE)
    short_range = grouped(repulsion_kernel, targets, (gather_local(extended, neighbors),)).reshape(
        3, atom_dev
    )
    centroid = lax.psum(coords, "bead") / beads
    with_charge = jnp.concatenate([centroid, charges[None]], axis=0)
    cent_ext = extended_2(with_charge, (("space", 1),), rim_width)
    cent_tiles = centroid.reshape(3, tiles_domain, TILE)
    cent_sources = gather_local(cent_ext[:3], neighbors)
    charge_sources = gather_local(cent_ext[3:], neighbors)
    permanent = grouped(charge_kernel, cent_tiles, (cent_sources, charge_sources)).reshape(
        3, atom_dev
    )

    def induced(dipole_all):
        wide_dip = extended_2(dipole_all, (("space", 1),), rim_width)
        field = grouped(
            dipole_kernel, cent_tiles, (cent_sources, gather_local(wide_dip, neighbors))
        )
        return field.reshape(3, atom_dev)

    domain_dip = polarizability[None] * permanent
    for sweep_index in range(ITERS):
        domain_dip = polarizability[None] * (permanent + induced(domain_dip))
    pulled = charges[None] * induced(domain_dip)
    dipoles = lax.dynamic_slice_in_dim(domain_dip, own_start * TILE, own_tiles * TILE, 1)
    forces = (short_range + spring + pulled)[None]
    return (forces, dipoles)


def solution(mesh):
    in_specs = (P("bead", None, "space"), P("space"), P("space"), P("space"), P("space", None))
    out_specs = (P("bead", None, "space"), P(None, ("space", "bead")))
    return jax.shard_map(
        per_device, mesh=mesh, in_specs=in_specs, out_specs=out_specs, check_vma=False
    )
```

profile of v0, /device:TPU:7, one launch (start us, length us, event | category | flops | bytes accessed | tf_op | source)
XLA Modules:
  0.0 1015.9 jit_solution(263732601985356042)
XLA Ops:
  8.3 2.5 collective-permute-start
  11.6 3.4 collective-permute-done.1
  15.9 145.2 %all-reduce.2.cloned.1.call-done = f32[3,16384]{1,0:T(4,128)} async-done(((f32[3,16384]{1,0:T(4,128)}), f32[3,16384]{1,0:T(4,128)}) %all-reduce.2.cloned.1.call-update) | async-done | bytes 196624 | tf_op jit(solution)/shard_map/psum | solution.py:89
  162.8 5.3 collective-permute-start.4
  169.2 3.6 gather_fusion.1
  173.3 2.8 gather_fusion
  177.1 8.0 gather_fusion.2
  185.1 3.6 fusion.29
  188.7 1.8 reshape_reshape.50
  192.1 87.0 %while.61 = (s32[]{:T(128)}, f32[32,3,4,128]{3,2,1,0:T(4,128)S(1)}, f32[32,3,4,128]{3,2,1,0:T(4,128)S(1)}, f32[32,3,4,1024]{3,2,1,0:T(4,128)}, f32[32,1,4,1024]{3,2,1,0:T(4,128)S(1)}, /*index=5*/s32[]{:T(128)}) while((s32[]{:T(128)}, f32[32,3,4,128]{3,2,1,0:T(4,128)S(1)}, f32[32,3,4,128]{3,2,1,0:T(4,128)S(1)}, f32[32,3,4,1024]{3,2,1,0:T(4,128)}, ...), condition=%wide.region_8.10_spmd, body=%wide.region_5.9_spmd.sunk | while | flops 9959938 | bytes 8677469 | solution.py:62
  279.4 3.0 collective-permute-start.6
  283.1 3.5 collective-permute-done.7
  286.7 3.6 gather_fusion.3
  291.7 1.8 reshape_reshape.52
  293.5 141.8 %while.62 = (s32[]{:T(128)}, f32[32,3,4,128]{3,2,1,0:T(4,128)S(1)}, f32[32,3,4,128]{3,2,1,0:T(4,128)S(1)}, f32[32,3,4,1024]{3,2,1,0:T(4,128)}, f32[32,3,4,1024]{3,2,0,1:T(4,128)S(1)}, /*index=5*/s32[]{:T(128)}) while((s32[]{:T(128)}, f32[32,3,4,128]{3,2,1,0:T(4,128)S(1)}, f32[32,3,4,128]{3,2,1,0:T(4,128)S(1)}, ...), condition=%wide.region_13.15_spmd, body=%wide.region_9.14_spmd.sunk | while | flops 15739394 | bytes 17262684 | solution.py:62
  336.2 1.6 fusion.51
  436.5 4.4 collective-permute-start.3
  441.0 3.6 gather_fusion.4
  446.0 1.8 reshape_reshape.54
  447.8 141.8 %while.63 = (s32[]{:T(128)}, f32[32,3,4,128]{3,2,1,0:T(4,128)S(1)}, f32[32,3,4,128]{3,2,1,0:T(4,128)S(1)}, f32[32,3,4,1024]{3,2,1,0:T(4,128)}, f32[32,3,4,1024]{3,2,0,1:T(4,128)S(1)}, /*index=5*/s32[]{:T(128)}) while((s32[]{:T(128)}, f32[32,3,4,128]{3,2,1,0:T(4,128)S(1)}, f32[32,3,4,128]{3,2,1,0:T(4,128)S(1)}, ...), condition=%wide.region_18.20_spmd, body=%wide.region_14.19_spmd.sunk | while | flops 15739394 | bytes 17262684 | solution.py:62
  590.0 3.1 collective-permute-start.10
  593.0 1.7 reshape_reshape.47
  594.7 2.6 collective-permute-done.11
  597.4 3.6 gather_fusion.5
  602.3 1.8 reshape_reshape.56
  604.1 141.8 %while.64 = (s32[]{:T(128)}, f32[32,3,4,128]{3,2,1,0:T(4,128)S(1)}, f32[32,3,4,128]{3,2,1,0:T(4,128)S(1)}, f32[32,3,4,1024]{3,2,1,0:T(4,128)}, f32[32,3,4,1024]{3,2,0,1:T(4,128)S(1)}, /*index=5*/s32[]{:T(128)}) while((s32[]{:T(128)}, f32[32,3,4,128]{3,2,1,0:T(4,128)S(1)}, f32[32,3,4,128]{3,2,1,0:T(4,128)S(1)}, ...), condition=%wide.region_23.25_spmd, body=%wide.region_19.24_spmd.sunk | while | flops 15739394 | bytes 17262684 | solution.py:62
  746.9 3.0 collective-permute-start.12
  749.9 107.9 %while.60 = (s32[]{:T(128)}, f32[32,3,4,128]{3,2,1,0:T(4,128)S(1)}, f32[32,3,4,128]{3,2,0,1:T(4,128)}, f32[32,3,4,1024]{3,2,0,1:T(4,128)}, s32[]{:T(128)}) while((s32[]{:T(128)}, f32[32,3,4,128]{3,2,1,0:T(4,128)S(1)}, f32[32,3,4,128]{3,2,0,1:T(4,128)}, f32[32,3,4,1024]{3,2,0,1:T(4,128)}, s32[]{:T(128)}) %tuple.164), condition=%wide.region_3.5_spmd, body=%wide.region_0.4_spmd.sunk | while | flops 9437186 | bytes 8628305 | solution.py:62
  857.9 3.6 gather_fusion.6
  862.9 1.8 reshape_reshape.58
  864.7 142.0 %while.65 = (s32[]{:T(128)}, f32[32,3,4,128]{3,2,1,0:T(4,128)S(1)}, f32[32,3,4,128]{3,2,1,0:T(4,128)S(1)}, f32[32,3,4,1024]{3,2,1,0:T(4,128)}, f32[32,3,4,1024]{3,2,0,1:T(4,128)S(1)}, /*index=5*/s32[]{:T(128)}) while((s32[]{:T(128)}, f32[32,3,4,128]{3,2,1,0:T(4,128)S(1)}, f32[32,3,4,128]{3,2,1,0:T(4,128)S(1)}, ...), condition=%wide.region_28.30_spmd, body=%wide.region_24.29_spmd.sunk | while | flops 15739394 | bytes 17262684 | solution.py:62
  1006.8 2.2 multiply_add_fusion
  (1402 shorter events, 769.6 us)
Async XLA Ops:
  7.2 160.9 %copy-start.7 = (s32[128,8]{0,1:T(8,128)S(1)}, s32[128,8]{0,1:T(8,128)}, u32[]{:S(2)}) copy-start(s32[128,8]{0,1:T(8,128)} %param.23) | copy-start | bytes 12292
  8.2 6.9 copy-start.1
  8.3 3.4 collective-permute-start
  10.7 4.3 collective-permute-start.1
  15.1 146.0 %all-reduce.2.cloned.1.call-start = ((), (), s32[]{:S(2)}) async-start(), calls=%async_computation | async-start | bytes 524288 | tf_op jit(solution)/shard_map/psum | solution.py:89
  162.8 10.2 collective-permute-start.4
  168.1 4.9 collective-permute-start.5
  169.2 3.8 copy-start.3
  190.5 1.3 copy-start.2
  190.5 1.3 copy-start.5
  192.1 87.2 %copy-start.4 = (f32[16384]{0:T(1024)S(1)}, f32[16384]{0:T(1024)}, u32[]{:S(2)}) copy-start(f32[16384]{0:T(1024)} %param.21) | copy-start | bytes 196612
  279.4 3.8 collective-permute-start.6
  282.3 4.3 collective-permute-start.7
  435.6 5.3 collective-permute-start.8
  435.7 5.3 collective-permute-start.9
  436.1 570.7 %collective-permute-start.2 = (f32[1,3,16384]{2,0,1:T(1,128)}, f32[1,3,16384]{2,0,1:T(1,128)S(1)}, u32[]{:S(2)}, u32[]{:S(2)}) collective-permute-start(f32[1,3,16384]{2,0,1:T(1,128)} %param.19), channel_id=1, source_target_pairs={{0,8},{8,16},{16,24},{24,32},{32,40},{40,48},{48,56},{56,64},{64,7... | collective-permute-start | bytes 589832 | tf_op jit(solution)/shard_map/ppermute | solution.py:24
  436.5 570.3 %collective-permute-start.3 = (f32[1,3,16384]{2,0,1:T(1,128)}, f32[1,3,16384]{2,0,1:T(1,128)}, u32[]{:S(2)}, u32[]{:S(2)}) collective-permute-start(f32[1,3,16384]{2,0,1:T(1,128)} %param.19), channel_id=1, source_target_pairs={{8,0},{16,8},{24,16},{32,24},{40,32},{48,40},{56,48},{64,56},{72,6... | collective-permute-start | bytes 589832 | tf_op jit(solution)/shard_map/ppermute | solution.py:25
  447.8 145.2 %copy-start.6 = (f32[16384]{0:T(1024)S(1)}, f32[16384]{0:T(1024)}, u32[]{:S(2)}) copy-start(f32[16384]{0:T(1024)} %param.22) | copy-start | bytes 196612
  589.7 3.4 copy-start
  590.0 4.7 collective-permute-start.10
  593.0 4.3 collective-permute-start.11
  746.9 111.0 %collective-permute-start.13 = (f32[3,512]{1,0:T(4,128)S(1)}, f32[3,512]{1,0:T(4,128)S(1)}, u32[]{:S(2)}, u32[]{:S(2)}) collective-permute-start(f32[3,512]{1,0:T(4,128)S(1)} %get-tuple-element.309), channel_id=1, source_target_pairs={{1,0},{2,1},{3,2},{4,3},{5,4},{6,5},{7,6},{0,7},{9,8},{10,9},{11,1... | collective-permute-start | bytes 18440 | tf_op jit(solution)/shard_map/ppermute | solution.py:25
  746.9 111.0 %collective-permute-start.12 = (f32[3,512]{1,0:T(4,128)S(1)}, f32[3,512]{1,0:T(4,128)S(1)}, u32[]{:S(2)}, u32[]{:S(2)}) collective-permute-start(f32[3,512]{1,0:T(4,128)S(1)} %get-tuple-element.310), channel_id=1, source_target_pairs={{0,1},{1,2},{2,3},{3,4},{4,5},{5,6},{6,7},{7,0},{8,9},{9,10},{10,1... | collective-permute-start | bytes 18440 | tf_op jit(solution)/shard_map/ppermute | solution.py:24
Sparse Core Ops, SparseCore 0:
  19.4 141.6 all-reduce.1
where the time goes:
time: 1030 us; the launch traced here: 1020 us
  other arithmetic  587 us (57%)
  local copies, waits for them, and re-layouts  227 us (22%)
  waiting for transfers between devices  156 us (15%)
  starting transfers between devices  22.1 us (2%)
  between operations  14.6 us (1%)
    reduce_sum x128, other arithmetic, dipole_kernel(): jnp.sum(weight[None] * (0.25 * displace * projected[None] - 0.5 * spread_...  199 us
    psum x1, waiting for transfers between devices, per_device(): centroid = lax.psum(coords, 'bead') / beads  145 us
    reduce_sum x128, other arithmetic, dipole_kernel(): weight = jnp.exp(-0.25 * jnp.sum(displace * displace, axis=0))  135 us
    exp x128, other arithmetic, dipole_kernel(): weight = jnp.exp(-0.25 * jnp.sum(displace * displace, axis=0))  119 us
    sub x256, local copies, waits for them, and re-layouts, dipole_kernel(): displace = targets[:, :, :, None] - sources[:, :, None, :]  105 us
    sub x64, local copies, waits for them, and re-layouts, repulsion_kernel(): displace = targets[:, :, :, None] - sources[:, :, None, :]  48 us
    gather x8, local copies, waits for them, and re-layouts, gather_local(): picked = jnp.take(tiles, tile_rows, axis=1)  29.6 us
    reduce_sum x32, other arithmetic, repulsion_kernel(): return REPULSION * jnp.sum(weight[None] * displace, axis=3)  27.5 us
  transfers between devices with their start and end apart: 15, of which 5 were waited for; matrix products, arithmetic and copies ran while one was open for 55% of the time, Pallas kernels for 0%

commit v1 on v0

v1 whole, which is shorter than its diff:
```python
import functools
import math

import jax
import jax.numpy as jnp
from jax import lax
from jax.experimental import pallas as pl
from jax.experimental.pallas import tpu as pltpu
from jax.sharding import PartitionSpec as P

TILE = 128
NBR = 8
HALO_T = 4
ITERS = 3
LOG2E = 1.4426950408889634
REPULSION = 0.2
SPRING = 0.1
UNROLL = 4
PLAN = (32, 12, 12, 12, 12, 12, 36)
VMEM = pltpu.MemorySpace.VMEM
SMEM = pltpu.MemorySpace.SMEM


def cols(at, n=TILE):
    return pl.ds(pl.multiple_of(at * TILE, TILE), n)


def split3(x):
    hi = x.astype(jnp.bfloat16).astype(jnp.float32)
    rest = x - hi
    mid = rest.astype(jnp.bfloat16).astype(jnp.float32)
    return hi, mid, rest - mid


def short_kernel(tiles, first, nb_ref, ext_ref, after_ref, out_ref, src, tgt, acc):
    width = src.shape[1]
    x = ext_ref[:, first * TILE : first * TILE + width]
    hi, mid, low = split3(x)
    src[...] = jnp.concatenate([hi, mid, low, hi, mid, hi], 0).astype(jnp.bfloat16)
    row = lax.broadcasted_iota(jnp.int32, hi.shape, 0)
    xyz = row < 3
    hi_t = jnp.where(xyz, hi, jnp.where(row == 3, 1.0, 0.0))
    mid_t = jnp.where(xyz, mid, 0.0)
    low_t = jnp.where(xyz, low, 0.0)
    tgt[...] = jnp.concatenate([hi_t, hi_t, hi_t, mid_t, mid_t, low_t], 0).astype(jnp.bfloat16)

    def finish(n, slot):
        sums = [
            jnp.sum(jnp.transpose(acc[slot, c]), axis=0, keepdims=True) for c in range(4)
        ]
        own = ext_ref[:, cols(n + first + HALO_T)]
        fade = (REPULSION / math.sqrt(LOG2E)) * jnp.exp2(own[3:4])
        pull = jnp.concatenate([sums[1], sums[2], sums[3]], 0)
        out_ref[:, cols(n)] = fade * (own[:3] * sums[0] - pull)

    def body(step, carry):
        for s in range(UNROLL):
            finish(jnp.maximum((step - 1) * UNROLL, 0) + s, s)
        for s in range(UNROLL):
            n = step * UNROLL + s
            lhs = tgt[:, cols(n + HALO_T)]
            at = [nb_ref[n + first, k] - first for k in range(NBR)]
            rows = [
                [
                    jnp.broadcast_to(ext_ref[c : c + 1, cols(at[k] + first)], (8, TILE))
                    for c in range(3)
                ]
                for k in range(NBR)
            ]
            expo = []
            for k in range(0, NBR, 2):
                rhs = jnp.concatenate([src[:, cols(at[k])], src[:, cols(at[k + 1])]], 1)
                expo.append(
                    lax.dot_general(
                        lhs, rhs, (((0,), (0,)), ((), ())), preferred_element_type=jnp.float32
                    )
                )
            for g in range(0, TILE, 8):
                total = None
                for k in range(NBR):
                    half = (k % 2) * TILE
                    u = jnp.exp2(expo[k // 2][g : g + 8, half : half + TILE])
                    parts = [u, u * rows[k][0], u * rows[k][1], u * rows[k][2]]
                    total = parts if k == 0 else [a + b for a, b in zip(total, parts)]
                for c in range(4):
                    acc[s, c, g : g + 8, :] = total[c]
        return carry

    steps = tiles // UNROLL
    for s in range(UNROLL):
        for c in range(4):
            acc[s, c] = jnp.zeros((TILE, TILE), jnp.float32)
    lax.fori_loop(0, steps, body, 0)
    for s in range(UNROLL):
        finish((steps - 1) * UNROLL + s, s)


def short_range(ext8, neighbors, first, tiles, after):
    width = (tiles + 2 * HALO_T) * TILE
    pairs = tiles * TILE * NBR * TILE
    return pl.pallas_call(
        functools.partial(short_kernel, tiles, first),
        out_shape=jax.ShapeDtypeStruct((3, tiles * TILE), jnp.float32),
        in_specs=[
            pl.BlockSpec(memory_space=SMEM),
            pl.BlockSpec(memory_space=VMEM),
            pl.BlockSpec(memory_space=pl.ANY),
        ],
        out_specs=pl.BlockSpec(memory_space=VMEM),
        scratch_shapes=[
            pltpu.VMEM((48, width), jnp.bfloat16),
            pltpu.VMEM((48, width), jnp.bfloat16),
            pltpu.VMEM((UNROLL, 4, TILE, TILE), jnp.float32),
        ],
        cost_estimate=pl.CostEstimate(
            flops=pairs * 100, bytes_accessed=4 * 11 * width, transcendentals=pairs
        ),
        compiler_params=pltpu.CompilerParams(vmem_limit_bytes=16 << 20),
        name="short_range",
    )(neighbors, ext8, after)


def centre_kernel(mode, own_tiles, nb_ref, *refs):
    ins, (out_ref, win, spread, acc) = refs, refs[-4:]
    size = own_tiles * TILE
    if mode == "permanent":
        before, own, after, charge, alpha = ins[:5]
    else:
        before, own, after, dip_b, dip_o, dip_a, scale = ins[:7]
    parts = (before, own, after)
    for p in range(3):
        win[0:3, p * size : (p + 1) * size] = parts[p][...]
    if mode == "permanent":
        win[3:4, :] = charge[...]
    else:
        for p, dip in enumerate((dip_b, dip_o, dip_a)):
            win[3:6, p * size : (p + 1) * size] = dip[0:3, :]

    def body(t):
        for c in range(3):
            line = win[c : c + 1, (t + HALO_T) * TILE : (t + HALO_T + 1) * TILE]
            spread[t, c] = jnp.transpose(jnp.broadcast_to(line, (TILE, TILE)))
        at = [nb_ref[t, k] for k in range(NBR)]
        wide = 4 if mode == "permanent" else 6
        rows = [
            [jnp.broadcast_to(win[c : c + 1, cols(at[k])], (8, TILE)) for c in range(wide)]
            for k in range(NBR)
        ]
        for g in range(0, TILE, 8):
            me = [spread[t, c, g : g + 8, :] for c in range(3)]
            total = None
            for k in range(NBR):
                d = [me[c] - rows[k][c] for c in range(3)]
                r2 = d[0] * d[0] + d[1] * d[1] + d[2] * d[2]
                w = jnp.exp2((-0.25 * LOG2E) * r2)
                if mode == "permanent":
                    w = w * rows[k][3]
                    add = [w * d[c] for c in range(3)]
                else:
                    m = rows[k][3:6]
                    p = 0.25 * (d[0] * m[0] + d[1] * m[1] + d[2] * m[2])
                    add = [w * (p * d[c] - 0.5 * m[c]) for c in range(3)]
                total = add if k == 0 else [a + b for a, b in zip(total, add)]
            for c in range(3):
                acc[t, c, g : g + 8, :] = total[c]
        here = slice(t * TILE, (t + 1) * TILE)
        for c in range(3):
            s = jnp.sum(jnp.transpose(acc[t, c]), axis=0, keepdims=True)
            if mode == "permanent":
                out_ref[c : c + 1, here] = alpha[:, here] * s
                out_ref[3 + c : 4 + c, here] = s
            elif mode == "dipole":
                out_ref[c : c + 1, here] = scale[:, here] * (ins[7][3 + c : 4 + c, here] + s)
            else:
                line = scale[:, here] * s
                out_ref[:, c : c + 1, here] = jnp.broadcast_to(line, (out_ref.shape[0], 1, TILE))

    for t in range(own_tiles):
        body(t)


def centre(mode, copies, after, nb, *arrays):
    size = arrays[0].shape[1]
    shape = {"permanent": (6, size), "dipole": (3, size), "pulled": (copies, 3, size)}[mode]
    pairs = size * NBR * TILE
    return pl.pallas_call(
        functools.partial(centre_kernel, mode, size // TILE),
        out_shape=jax.ShapeDtypeStruct(shape, jnp.float32),
        in_specs=[pl.BlockSpec(memory_space=SMEM)]
        + [pl.BlockSpec(memory_space=VMEM)] * len(arrays)
        + [pl.BlockSpec(memory_space=pl.ANY)] * len(after),
        out_specs=pl.BlockSpec(memory_space=VMEM),
        scratch_shapes=[
            pltpu.VMEM((8, 3 * size), jnp.float32),
            pltpu.VMEM((HALO_T, 3, TILE, TILE), jnp.float32),
            pltpu.VMEM((HALO_T, 3, TILE, TILE), jnp.float32),
        ],
        cost_estimate=pl.CostEstimate(
            flops=pairs * 100, bytes_accessed=4 * 24 * size, transcendentals=pairs
        ),
        compiler_params=pltpu.CompilerParams(vmem_limit_bytes=16 << 20),
    )(nb, *arrays, *after)


def pack_kernel(order, pos_ref, out_ref):
    size = out_ref.shape[2]
    for b, share in enumerate(order):
        out_ref[b] = pos_ref[:, share * size : (share + 1) * size]


def pack(order, coords):
    size = coords.shape[1] // len(order)
    return pl.pallas_call(
        functools.partial(pack_kernel, order),
        out_shape=jax.ShapeDtypeStruct((len(order), 3, size), jnp.float32),
        in_specs=[pl.BlockSpec(memory_space=VMEM)],
        out_specs=pl.BlockSpec(memory_space=VMEM),
        compiler_params=pltpu.CompilerParams(vmem_limit_bytes=8 << 20),
        name="pack",
    )(coords)


def total_kernel(order, plan, pos, last, following, masses, every, *refs):
    short, out_ref = refs[:-1], refs[-1]
    size = every.shape[2]
    for b, share in enumerate(order):
        here = slice(share * size, (share + 1) * size)
        at, piece = share * size // TILE, 0
        while at >= plan[piece]:
            at, piece = at - plan[piece], piece + 1
        spring = (SPRING * masses[:, here]) * (
            last[:, here] + following[:, here] - 2.0 * pos[:, here]
        )
        force = short[piece][:, at * TILE : at * TILE + size] + spring + every[b]
        for c in range(3):
            out_ref[c, :, here] = force[c : c + 1]


def total(order, plan, *arrays):
    width = arrays[0].shape[1]
    return pl.pallas_call(
        functools.partial(total_kernel, order, plan),
        out_shape=jax.ShapeDtypeStruct((3, 1, width), jnp.float32),
        in_specs=[pl.BlockSpec(memory_space=VMEM)] * len(arrays),
        out_specs=pl.BlockSpec(memory_space=VMEM),
        compiler_params=pltpu.CompilerParams(vmem_limit_bytes=8 << 20),
        name="total",
    )(*arrays)


def per_device(beads, spaces, positions, charges, polarizability, masses, neighbors):
    coords = positions[0]
    atom_dev = coords.shape[1]
    rim = HALO_T * TILE
    size = atom_dev // beads
    own_tiles = size // TILE
    assert size == rim
    across = math.gcd(beads, 8)
    bead = lax.axis_index("bead")

    def share_of(b):
        row, at = b // across, b % across
        return row * across + (across - 1 - at if row % 2 else at)

    order = [share_of(b) for b in range(beads)]
    row, at = bead // across, bead % across
    share = row * across + jnp.where(row % 2 == 1, across - 1 - at, at)
    start = share * size

    def place(g):
        return share_of(g % beads) * spaces + g // beads

    count = beads * spaces
    fore = [(place(g), place((g + 1) % count)) for g in range(count)]
    back = [(j, i) for i, j in fore]
    both = ("bead", "space")

    def around(x):
        return lax.ppermute(x, both, fore), x, lax.ppermute(x, both, back)

    up = [(s, (s + 1) % spaces) for s in range(spaces)]
    down = [(j, i) for i, j in up]
    held = jnp.concatenate([coords, charges[None]], 0)
    before = lax.ppermute(held[:, atom_dev - rim :], "space", up)
    after = lax.ppermute(held[:, :rim], "space", down)
    ext = jnp.concatenate([before, held, after], 1)
    x = ext[:3] * math.sqrt(LOG2E)
    ext8 = jnp.concatenate(
        [x, -0.5 * jnp.sum(x * x, 0, keepdims=True), jnp.zeros((4, x.shape[1]), x.dtype)], 0
    )
    near_charge = lax.dynamic_slice(ext[3:4], (0, start), (1, size + 2 * rim))

    shares = pack(order, coords)
    cent = jnp.sum(lax.all_to_all(shares, "bead", 0, 0), axis=0) / beads

    own_rows = lax.dynamic_slice(neighbors, (share * own_tiles, 0), (own_tiles, NBR))
    nb = own_rows - share * own_tiles
    alpha = lax.dynamic_slice(polarizability, (start,), (size,))[None]
    charge = lax.dynamic_slice(charges, (start,), (size,))[None]

    tiles = atom_dev // TILE
    plan = [n * tiles // sum(PLAN) for n in PLAN]
    short = []

    def fill(after):
        first = sum(plan[: len(short)])
        short.append(short_range(ext8, neighbors, first, plan[len(short)], after))
        return short[-1]

    wait = fill(shares)
    cent, wait = lax.optimization_barrier((cent, wait))
    c3 = around(cent)
    wait = fill(cent)
    state = centre("permanent", beads, (wait,), nb, *c3, near_charge, alpha)

    turn = [(b, (b + 1) % beads) for b in range(beads)]
    turn_back = [(j, i) for i, j in turn]
    late, state = lax.optimization_barrier((coords, state))
    last = lax.ppermute(late, "bead", turn)
    following = lax.ppermute(late, "bead", turn_back)
    dip = state[:3]
    for sweep in range(ITERS):
        d3 = around(dip)
        hold = (fill(dip), last, following) if sweep == 1 else (fill(dip),)
        dip = centre("dipole", beads, hold, nb, *c3, *d3, alpha, state)
    d3 = around(dip)
    pulled = centre("pulled", beads, (fill(dip),), nb, *c3, *d3, charge)
    fill(pulled)
    every = lax.all_to_all(pulled, "bead", 0, 0)
    forces = total(order, plan, coords, last, following, masses[None], every, *short)
    forces = forces.transpose(1, 0, 2)
    dipoles = lax.ppermute(dip, "bead", [(b, share_of(b)) for b in range(beads)])
    return forces, dipoles


def solution(mesh):
    in_specs = (P("bead", None, "space"), P("space"), P("space"), P("space"), P("space", None))
    out_specs = (P("bead", None, "space"), P(None, ("space", "bead")))

    def body(*arrays):
        return per_device(mesh.shape["bead"], mesh.shape["space"], *arrays)

    return jax.shard_map(
        body, mesh=mesh, in_specs=in_specs, out_specs=out_specs, check_vma=False
    )
```

time: 1030 us -> 118 us (0.11)
  the two profiles are of different devices: /device:TPU:7 before, /device:TPU:40 now
where the time goes in v1:
time: 118 us
  Pallas kernels  60.6 us (51%)
  starting transfers between devices  49.3 us (42%)
  local copies, waits for them, and re-layouts  3.4 us (3%)
  waiting for transfers between devices  3.16 us (3%)
    pallas_call x7, Pallas kernels, short_range(): pl.pallas_call(functools.partial(short_kernel, tiles, first), out_shape=j...  43.6 us
    pallas_call x5, Pallas kernels, centre(): pl.pallas_call(functools.partial(centre_kernel, mode, size // TILE), out_...  15.4 us
    all_to_all x1, starting transfers between devices, per_device(): every = lax.all_to_all(pulled, 'bead', 0, 0)  14.9 us
    ppermute x10, starting transfers between devices, around(): return (lax.ppermute(x, both, fore), x, lax.ppermute(x, both, back))  12.5 us
    all_to_all x1, starting transfers between devices, per_device(): cent = jnp.sum(lax.all_to_all(shares, 'bead', 0, 0), axis=0) / beads  11.2 us
    ppermute x1, starting transfers between devices, per_device(): lax.ppermute(dip, 'bead', [(b, share_of(b)) for b in range(beads)])  5.65 us
    ppermute x1, waiting for transfers between devices, per_device(): lax.ppermute(dip, 'bead', [(b, share_of(b)) for b in range(beads)])  3.03 us
    ppermute x1, starting transfers between devices, per_device(): after = lax.ppermute(held[:, :rim], 'space', down)  2.94 us
  transfers between devices with their start and end apart: 17, of which 2 were waited for; matrix products, arithmetic and copies ran while one was open for 1% of the time, Pallas kernels for 40%

profile of v1, /device:TPU:40, one launch (start us, length us, event | category | flops | bytes accessed | tf_op | source)
XLA Modules:
  0.0 118.1 jit_solution(13858644083976742092)
XLA Ops:
  0.6 1.1 copy.17
  1.8 2.9 %collective-permute-start.1 = (f32[4,512]{1,0:T(4,128)S(1)}, f32[4,512]{1,0:T(4,128)S(1)}, u32[]{:S(2)}, u32[]{:S(2)}) collective-permute-start(f32[4,512]{1,0:T(4,128)S(1)} %get-tuple-element.9), channel_id=1, source_target_pairs={{1,0},{2,1},{3,2},{4,3},{5,4},{6,5},{7,6},{0,7},{9,8},{10,9},{11,1... | collective-permute-start | bytes 24584 | tf_op jit(solution)/shard_map/ppermute | solution.py:285
  4.7 0.7 pack.1.after_ref
  5.5 11.2 %all-to-all-start = ((f32[32,3,512]{2,1,0:T(4,128)}), f32[32,3,512]{2,1,0:T(4,128)S(1)}, u32[]{:S(2)}, u32[]{:S(2)}) async-start(f32[32,3,512]{2,1,0:T(4,128)} %pack.1.after_ref), calls=%async_computation | async-start | bytes 524288 | tf_op jit(solution)/shard_map/all_to_all | solution.py:294
  16.8 0.7 copy-done.2
  17.7 0.8 dynamic_slice.14
  18.9 9.4 %short_range.7.refs_0_ = f32[3,4096]{1,0:T(4,128)S(1)} custom-call(s32[128,8]{1,0:T(8,128)S(1)} %copy.7.nb_ref, f32[8,17408]{1,0:T(8,128)S(1)} %maximum_maximum_fusion.ext_ref, f32[32,3,512]{2,1,0:T(4,128)} %pack.1.after_ref), custom_call_target="tpu_custom_call" | custom-call | flops 419430400 | bytes 225280 | tf_op jit(solution)/shard_map/short_range/pallas_call | solution.py:101
  28.5 1.5 %collective-permute-start.3 = (f32[3,512]{1,0:T(4,128)S(1)}, f32[3,512]{1,0:T(4,128)S(1)}, u32[]{:S(2)}, u32[]{:S(2)}) collective-permute-start(f32[3,512]{1,0:T(4,128)S(1)} %broadcast_multiply_fusion.1.after_ref.refs_1_), channel_id=1, source_target_pairs={{8,0},{16,8},{24,16},{32,24},{40,32},{48,40},{56,48},{120,56},{112... | collective-permute-start | bytes 18440 | tf_op jit(solution)/shard_map/ppermute | solution.py:279
  30.1 0.6 collective-permute-start.2
  30.7 4.8 %short_range.8.refs_5_.refs_1_ = f32[3,1536]{1,0:T(4,128)S(1)} custom-call(s32[128,8]{1,0:T(8,128)S(1)} %copy.7.nb_ref, f32[8,17408]{1,0:T(8,128)S(1)} %maximum_maximum_fusion.ext_ref, f32[3,512]{1,0:T(4,128)S(1)} %broadcast_multiply_fusion.1.after_ref.refs_1_), custom_call_target="tpu_custom_call" | custom-call | flops 157286400 | bytes 112640 | tf_op jit(solution)/shard_map/short_range/pallas_call | solution.py:101
  35.5 2.1 %shard_map.68.refs_7_ = f32[6,512]{1,0:T(8,128)S(1)} custom-call(s32[4,8]{1,0:T(4,128)S(1)} %dynamic-slice_subtract_fusion.nb_ref, f32[3,512]{1,0:T(4,128)S(1)} %collective-permute-done.2.refs_0_, f32[3,512]{1,0:T(4,128)S(1)} %broadcast_multiply_fusion.1.after_ref.refs_1_, f32[3,512]{1,0:T(4,128)S(1)} %collective-permute-done.3.refs_2_, ...), custom_call_target="tpu_custom_call" | custom-call | flops 52428800 | bytes 49152 | tf_op jit(solution)/shard_map/pallas_call | solution.py:186
  37.6 0.6 collective-permute-start.5
  38.2 1.5 %collective-permute-start.4 = (f32[3,16384]{1,0:T(4,128)S(1)}, f32[3,16384]{1,0:T(4,128)S(1)}, u32[]{:S(2)}, u32[]{:S(2)}) collective-permute-start(f32[3,16384]{1,0:T(4,128)S(1)} %bitcast.14), channel_id=1, source_target_pairs={{0,8},{8,16},{16,24},{24,32},{32,40},{40,48},{48,56},{56,64},{64,7... | collective-permute-start | bytes 589832 | tf_op jit(solution)/shard_map/ppermute | solution.py:319
  39.8 1.7 %collective-permute-start.7 = (f32[3,512]{1,0:T(4,128)S(1)}, f32[3,512]{1,0:T(4,128)S(1)}, u32[]{:S(2)}, u32[]{:S(2)}) collective-permute-start(f32[3,512]{1,0:T(4,128)S(1)} %slice.19.after_ref.refs_4_), channel_id=1, source_target_pairs={{8,0},{16,8},{24,16},{32,24},{40,32},{48,40},{56,48},{120,56},{112... | collective-permute-start | bytes 18440 | tf_op jit(solution)/shard_map/ppermute | solution.py:279
  41.5 0.4 collective-permute-start.6
  41.8 4.8 %short_range.9.refs_8_.refs_2_ = f32[3,1536]{1,0:T(4,128)S(1)} custom-call(s32[128,8]{1,0:T(8,128)S(1)} %copy.7.nb_ref, f32[8,17408]{1,0:T(8,128)S(1)} %maximum_maximum_fusion.ext_ref, f32[3,512]{1,0:T(4,128)S(1)} %slice.19.after_ref.refs_4_), custom_call_target="tpu_custom_call" | custom-call | flops 157286400 | bytes 112640 | tf_op jit(solution)/shard_map/short_range/pallas_call | solution.py:101
  46.7 3.1 %shard_map.69.after_ref.refs_4_ = f32[3,512]{1,0:T(4,128)S(1)} custom-call(s32[4,8]{1,0:T(4,128)S(1)} %dynamic-slice_subtract_fusion.nb_ref, f32[3,512]{1,0:T(4,128)S(1)} %collective-permute-done.2.refs_0_, f32[3,512]{1,0:T(4,128)S(1)} %broadcast_multiply_fusion.1.after_ref.refs_1_, f32[3,512]{1,0:T(4,128)S(1)} %collective-permute-done.3.refs_2_, ...), custom_call_target="tpu_custom_call" | custom-call | flops 52428800 | bytes 49152 | tf_op jit(solution)/shard_map/pallas_call | solution.py:186
  49.8 2.9 %collective-permute-start.9 = (f32[3,512]{1,0:T(4,128)S(1)}, f32[3,512]{1,0:T(4,128)S(1)}, u32[]{:S(2)}, u32[]{:S(2)}) collective-permute-start(f32[3,512]{1,0:T(4,128)S(1)} %shard_map.69.after_ref.refs_4_), channel_id=1, source_target_pairs={{8,0},{16,8},{24,16},{32,24},{40,32},{48,40},{56,48},{120,56},{112... | collective-permute-start | bytes 18440 | tf_op jit(solution)/shard_map/ppermute | solution.py:279
  52.7 4.8 %short_range.10.refs_8_.refs_3_ = f32[3,1536]{1,0:T(4,128)S(1)} custom-call(s32[128,8]{1,0:T(8,128)S(1)} %copy.7.nb_ref, f32[8,17408]{1,0:T(8,128)S(1)} %maximum_maximum_fusion.ext_ref, f32[3,512]{1,0:T(4,128)S(1)} %shard_map.69.after_ref.refs_4_), custom_call_target="tpu_custom_call" | custom-call | flops 157286400 | bytes 112640 | tf_op jit(solution)/shard_map/short_range/pallas_call | solution.py:101
  57.5 3.1 %shard_map.70.after_ref.refs_4_ = f32[3,512]{1,0:T(4,128)S(1)} custom-call(s32[4,8]{1,0:T(4,128)S(1)} %dynamic-slice_subtract_fusion.nb_ref, f32[3,512]{1,0:T(4,128)S(1)} %collective-permute-done.2.refs_0_, f32[3,512]{1,0:T(4,128)S(1)} %broadcast_multiply_fusion.1.after_ref.refs_1_, f32[3,512]{1,0:T(4,128)S(1)} %collective-permute-done.3.refs_2_, ...), custom_call_target="tpu_custom_call" | custom-call | flops 52428800 | bytes 49152 | tf_op jit(solution)/shard_map/pallas_call | solution.py:186
  60.6 2.1 %collective-permute-start.11 = (f32[3,512]{1,0:T(4,128)S(1)}, f32[3,512]{1,0:T(4,128)S(1)}, u32[]{:S(2)}, u32[]{:S(2)}) collective-permute-start(f32[3,512]{1,0:T(4,128)S(1)} %shard_map.70.after_ref.refs_4_), channel_id=1, source_target_pairs={{8,0},{16,8},{24,16},{32,24},{40,32},{48,40},{56,48},{120,56},{112... | collective-permute-start | bytes 18440 | tf_op jit(solution)/shard_map/ppermute | solution.py:279
  62.7 4.8 %short_range.11.refs_8_.refs_4_ = f32[3,1536]{1,0:T(4,128)S(1)} custom-call(s32[128,8]{1,0:T(8,128)S(1)} %copy.7.nb_ref, f32[8,17408]{1,0:T(8,128)S(1)} %maximum_maximum_fusion.ext_ref, f32[3,512]{1,0:T(4,128)S(1)} %shard_map.70.after_ref.refs_4_), custom_call_target="tpu_custom_call" | custom-call | flops 157286400 | bytes 112640 | tf_op jit(solution)/shard_map/short_range/pallas_call | solution.py:101
  67.6 3.1 %shard_map.71.after_ref.refs_4_ = f32[3,512]{1,0:T(4,128)S(1)} custom-call(s32[4,8]{1,0:T(4,128)S(1)} %dynamic-slice_subtract_fusion.nb_ref, f32[3,512]{1,0:T(4,128)S(1)} %collective-permute-done.2.refs_0_, f32[3,512]{1,0:T(4,128)S(1)} %broadcast_multiply_fusion.1.after_ref.refs_1_, f32[3,512]{1,0:T(4,128)S(1)} %collective-permute-done.3.refs_2_, ...), custom_call_target="tpu_custom_call" | custom-call | flops 52428800 | bytes 49152 | tf_op jit(solution)/shard_map/pallas_call | solution.py:186
  70.7 3.3 %collective-permute-start.13 = (f32[3,512]{1,0:T(4,128)S(1)}, f32[3,512]{1,0:T(4,128)S(1)}, u32[]{:S(2)}, u32[]{:S(2)}) collective-permute-start(f32[3,512]{1,0:T(4,128)S(1)} %shard_map.71.after_ref.refs_4_), channel_id=1, source_target_pairs={{8,0},{16,8},{24,16},{32,24},{40,32},{48,40},{56,48},{120,56},{112... | collective-permute-start | bytes 18440 | tf_op jit(solution)/shard_map/ppermute | solution.py:279
  74.0 4.8 %short_range.12.refs_7_.refs_5_ = f32[3,1536]{1,0:T(4,128)S(1)} custom-call(s32[128,8]{1,0:T(8,128)S(1)} %copy.7.nb_ref, f32[8,17408]{1,0:T(8,128)S(1)} %maximum_maximum_fusion.ext_ref, f32[3,512]{1,0:T(4,128)S(1)} %shard_map.71.after_ref.refs_4_), custom_call_target="tpu_custom_call" | custom-call | flops 157286400 | bytes 112640 | tf_op jit(solution)/shard_map/short_range/pallas_call | solution.py:101
  78.8 3.9 %shard_map.72.after_ref = f32[32,3,512]{2,1,0:T(4,128)} custom-call(s32[4,8]{1,0:T(4,128)S(1)} %dynamic-slice_subtract_fusion.nb_ref, f32[3,512]{1,0:T(4,128)S(1)} %collective-permute-done.2.refs_0_, f32[3,512]{1,0:T(4,128)S(1)} %broadcast_multiply_fusion.1.after_ref.refs_1_, f32[3,512]{1,0:T(4,128)S(1)} %collective-permute-done.3.refs_2_, ...), custom_call_target="tpu_custom_call" | custom-call | flops 52428800 | bytes 49152 | tf_op jit(solution)/shard_map/pallas_call | solution.py:186
  82.7 14.9 %all-to-all-start.1 = ((f32[32,3,512]{2,1,0:T(4,128)}), f32[32,3,512]{2,1,0:T(4,128)S(1)}, u32[]{:S(2)}, u32[]{:S(2)}) async-start(f32[32,3,512]{2,1,0:T(4,128)} %shard_map.72.after_ref), calls=%async_computation.1 | async-start | bytes 524288 | tf_op jit(solution)/shard_map/all_to_all | solution.py:329
  97.6 5.6 %collective-permute-start.14 = (f32[3,512]{1,0:T(4,128)S(1)}, f32[3,512]{1,0:T(4,128)S(1)}, u32[]{:S(2)}, u32[]{:S(2)}) collective-permute-start(f32[3,512]{1,0:T(4,128)S(1)} %shard_map.71.after_ref.refs_4_), channel_id=1, source_target_pairs={{0,0},{8,8},{16,16},{24,24},{32,32},{40,40},{48,48},{56,56},{64,12... | collective-permute-start | bytes 18440 | tf_op jit(solution)/shard_map/ppermute | solution.py:332
  103.3 3.0 %collective-permute-done.14 = f32[3,512]{1,0:T(4,128)S(1)} collective-permute-done((f32[3,512]{1,0:T(4,128)S(1)}, f32[3,512]{1,0:T(4,128)S(1)}, u32[]{:S(2)}, u32[]{:S(2)}) %collective-permute-start.14) | collective-permute-done | bytes 6176 | tf_op jit(solution)/shard_map/ppermute | solution.py:332
  106.3 10.3 %short_range.13.refs_6_ = f32[3,4608]{1,0:T(4,128)S(1)} custom-call(s32[128,8]{1,0:T(8,128)S(1)} %copy.7.nb_ref, f32[8,17408]{1,0:T(8,128)S(1)} %maximum_maximum_fusion.ext_ref, f32[32,3,512]{2,1,0:T(4,128)} %shard_map.72.after_ref), custom_call_target="tpu_custom_call" | custom-call | flops 471859200 | bytes 247808 | tf_op jit(solution)/shard_map/short_range/pallas_call | solution.py:101
  116.7 0.8 total.1
  117.5 0.6 copy.19
  (39 shorter events, 1.1 us)
Async XLA Ops:
  0.6 1.1 copy-start.1
  1.8 16.7 %collective-permute-start = (f32[4,512]{1,0:T(4,128)S(1)}, f32[4,512]{1,0:T(4,128)S(1)}, u32[]{:S(2)}, u32[]{:S(2)}) collective-permute-start(f32[4,512]{1,0:T(4,128)S(1)} %get-tuple-element.8), channel_id=1, source_target_pairs={{0,1},{1,2},{2,3},{3,4},{4,5},{5,6},{6,7},{7,0},{8,9},{9,10},{10,1... | collective-permute-start | bytes 24584 | tf_op jit(solution)/shard_map/ppermute | solution.py:284
  1.8 16.6 %collective-permute-start.1 = (f32[4,512]{1,0:T(4,128)S(1)}, f32[4,512]{1,0:T(4,128)S(1)}, u32[]{:S(2)}, u32[]{:S(2)}) collective-permute-start(f32[4,512]{1,0:T(4,128)S(1)} %get-tuple-element.9), channel_id=1, source_target_pairs={{1,0},{2,1},{3,2},{4,3},{5,4},{6,5},{7,6},{0,7},{9,8},{10,9},{11,1... | collective-permute-start | bytes 24584 | tf_op jit(solution)/shard_map/ppermute | solution.py:285
  5.5 23.0 %all-to-all-start = ((f32[32,3,512]{2,1,0:T(4,128)}), f32[32,3,512]{2,1,0:T(4,128)S(1)}, u32[]{:S(2)}, u32[]{:S(2)}) async-start(f32[32,3,512]{2,1,0:T(4,128)} %pack.1.after_ref), calls=%async_computation | async-start | bytes 524288 | tf_op jit(solution)/shard_map/all_to_all | solution.py:294
  16.8 0.7 copy-start.2
  28.5 6.9 %collective-permute-start.3 = (f32[3,512]{1,0:T(4,128)S(1)}, f32[3,512]{1,0:T(4,128)S(1)}, u32[]{:S(2)}, u32[]{:S(2)}) collective-permute-start(f32[3,512]{1,0:T(4,128)S(1)} %broadcast_multiply_fusion.1.after_ref.refs_1_), channel_id=1, source_target_pairs={{8,0},{16,8},{24,16},{32,24},{40,32},{48,40},{56,48},{120,56},{112... | collective-permute-start | bytes 18440 | tf_op jit(solution)/shard_map/ppermute | solution.py:279
  30.1 5.4 %collective-permute-start.2 = (f32[3,512]{1,0:T(4,128)S(1)}, f32[3,512]{1,0:T(4,128)S(1)}, u32[]{:S(2)}, u32[]{:S(2)}) collective-permute-start(f32[3,512]{1,0:T(4,128)S(1)} %broadcast_multiply_fusion.1.after_ref.refs_1_), channel_id=1, source_target_pairs={{0,8},{8,16},{16,24},{24,32},{32,40},{40,48},{48,56},{56,120},{120... | collective-permute-start | bytes 18440 | tf_op jit(solution)/shard_map/ppermute | solution.py:279
  37.6 19.9 %collective-permute-start.5 = (f32[3,16384]{1,0:T(4,128)S(1)}, f32[3,16384]{1,0:T(4,128)S(1)}, u32[]{:S(2)}, u32[]{:S(2)}) collective-permute-start(f32[3,16384]{1,0:T(4,128)S(1)} %bitcast.13), channel_id=1, source_target_pairs={{8,0},{16,8},{24,16},{32,24},{40,32},{48,40},{56,48},{64,56},{72,6... | collective-permute-start | bytes 589832 | tf_op jit(solution)/shard_map/ppermute | solution.py:320
  38.2 19.3 %collective-permute-start.4 = (f32[3,16384]{1,0:T(4,128)S(1)}, f32[3,16384]{1,0:T(4,128)S(1)}, u32[]{:S(2)}, u32[]{:S(2)}) collective-permute-start(f32[3,16384]{1,0:T(4,128)S(1)} %bitcast.14), channel_id=1, source_target_pairs={{0,8},{8,16},{16,24},{24,32},{32,40},{40,48},{48,56},{56,64},{64,7... | collective-permute-start | bytes 589832 | tf_op jit(solution)/shard_map/ppermute | solution.py:319
  39.8 6.8 %collective-permute-start.7 = (f32[3,512]{1,0:T(4,128)S(1)}, f32[3,512]{1,0:T(4,128)S(1)}, u32[]{:S(2)}, u32[]{:S(2)}) collective-permute-start(f32[3,512]{1,0:T(4,128)S(1)} %slice.19.after_ref.refs_4_), channel_id=1, source_target_pairs={{8,0},{16,8},{24,16},{32,24},{40,32},{48,40},{56,48},{120,56},{112... | collective-permute-start | bytes 18440 | tf_op jit(solution)/shard_map/ppermute | solution.py:279
  41.5 5.2 %collective-permute-start.6 = (f32[3,512]{1,0:T(4,128)S(1)}, f32[3,512]{1,0:T(4,128)S(1)}, u32[]{:S(2)}, u32[]{:S(2)}) collective-permute-start(f32[3,512]{1,0:T(4,128)S(1)} %slice.19.after_ref.refs_4_), channel_id=1, source_target_pairs={{0,8},{8,16},{16,24},{24,32},{32,40},{40,48},{48,56},{56,120},{120... | collective-permute-start | bytes 18440 | tf_op jit(solution)/shard_map/ppermute | solution.py:279
  49.8 7.7 %collective-permute-start.9 = (f32[3,512]{1,0:T(4,128)S(1)}, f32[3,512]{1,0:T(4,128)S(1)}, u32[]{:S(2)}, u32[]{:S(2)}) collective-permute-start(f32[3,512]{1,0:T(4,128)S(1)} %shard_map.69.after_ref.refs_4_), channel_id=1, source_target_pairs={{8,0},{16,8},{24,16},{32,24},{40,32},{48,40},{56,48},{120,56},{112... | collective-permute-start | bytes 18440 | tf_op jit(solution)/shard_map/ppermute | solution.py:279
  52.7 4.8 %collective-permute-start.8 = (f32[3,512]{1,0:T(4,128)S(1)}, f32[3,512]{1,0:T(4,128)S(1)}, u32[]{:S(2)}, u32[]{:S(2)}) collective-permute-start(f32[3,512]{1,0:T(4,128)S(1)} %shard_map.69.after_ref.refs_4_), channel_id=1, source_target_pairs={{0,8},{8,16},{16,24},{24,32},{32,40},{40,48},{48,56},{56,120},{120... | collective-permute-start | bytes 18440 | tf_op jit(solution)/shard_map/ppermute | solution.py:279
  60.6 6.9 %collective-permute-start.11 = (f32[3,512]{1,0:T(4,128)S(1)}, f32[3,512]{1,0:T(4,128)S(1)}, u32[]{:S(2)}, u32[]{:S(2)}) collective-permute-start(f32[3,512]{1,0:T(4,128)S(1)} %shard_map.70.after_ref.refs_4_), channel_id=1, source_target_pairs={{8,0},{16,8},{24,16},{32,24},{40,32},{48,40},{56,48},{120,56},{112... | collective-permute-start | bytes 18440 | tf_op jit(solution)/shard_map/ppermute | solution.py:279
  62.7 4.8 %collective-permute-start.10 = (f32[3,512]{1,0:T(4,128)S(1)}, f32[3,512]{1,0:T(4,128)S(1)}, u32[]{:S(2)}, u32[]{:S(2)}) collective-permute-start(f32[3,512]{1,0:T(4,128)S(1)} %shard_map.70.after_ref.refs_4_), channel_id=1, source_target_pairs={{0,8},{8,16},{16,24},{24,32},{32,40},{40,48},{48,56},{56,120},{120... | collective-permute-start | bytes 18440 | tf_op jit(solution)/shard_map/ppermute | solution.py:279
  70.7 8.1 %collective-permute-start.13 = (f32[3,512]{1,0:T(4,128)S(1)}, f32[3,512]{1,0:T(4,128)S(1)}, u32[]{:S(2)}, u32[]{:S(2)}) collective-permute-start(f32[3,512]{1,0:T(4,128)S(1)} %shard_map.71.after_ref.refs_4_), channel_id=1, source_target_pairs={{8,0},{16,8},{24,16},{32,24},{40,32},{48,40},{56,48},{120,56},{112... | collective-permute-start | bytes 18440 | tf_op jit(solution)/shard_map/ppermute | solution.py:279
  74.0 4.9 %collective-permute-start.12 = (f32[3,512]{1,0:T(4,128)S(1)}, f32[3,512]{1,0:T(4,128)S(1)}, u32[]{:S(2)}, u32[]{:S(2)}) collective-permute-start(f32[3,512]{1,0:T(4,128)S(1)} %shard_map.71.after_ref.refs_4_), channel_id=1, source_target_pairs={{0,8},{8,16},{16,24},{24,32},{32,40},{40,48},{48,56},{56,120},{120... | collective-permute-start | bytes 18440 | tf_op jit(solution)/shard_map/ppermute | solution.py:279
  82.7 34.0 %all-to-all-start.1 = ((f32[32,3,512]{2,1,0:T(4,128)}), f32[32,3,512]{2,1,0:T(4,128)S(1)}, u32[]{:S(2)}, u32[]{:S(2)}) async-start(f32[32,3,512]{2,1,0:T(4,128)} %shard_map.72.after_ref), calls=%async_computation.1 | async-start | bytes 524288 | tf_op jit(solution)/shard_map/all_to_all | solution.py:329
  97.6 19.0 %copy-start = (f32[16384]{0:T(1024)S(1)}, f32[16384]{0:T(1024)}, u32[]{:S(2)}) copy-start(f32[16384]{0:T(1024)} %param.8) | copy-start | bytes 196612
  97.6 8.7 %collective-permute-start.14 = (f32[3,512]{1,0:T(4,128)S(1)}, f32[3,512]{1,0:T(4,128)S(1)}, u32[]{:S(2)}, u32[]{:S(2)}) collective-permute-start(f32[3,512]{1,0:T(4,128)S(1)} %shard_map.71.after_ref.refs_4_), channel_id=1, source_target_pairs={{0,0},{8,8},{16,16},{24,24},{32,32},{40,40},{48,48},{56,56},{64,12... | collective-permute-start | bytes 18440 | tf_op jit(solution)/shard_map/ppermute | solution.py:332

commit v2 on v1

--- a/solution.py
+++ b/solution.py
@@ -16,7 +16,7 @@
 REPULSION = 0.2
 SPRING = 0.1
 UNROLL = 4
-PLAN = (32, 12, 12, 12, 12, 12, 36)
+PLAN = (28, 12, 16, 12, 16, 12, 32)
 VMEM = pltpu.MemorySpace.VMEM
 SMEM = pltpu.MemorySpace.SMEM
 
@@ -32,7 +32,7 @@
     return hi, mid, rest - mid
 
 
-def short_kernel(tiles, first, nb_ref, ext_ref, after_ref, out_ref, src, tgt, acc):
+def short_kernel(tiles, first, nb_ref, ext_ref, after_ref, out_ref, src, tgt, acc, expo):
     width = src.shape[1]
     x = ext_ref[:, first * TILE : first * TILE + width]
     hi, mid, low = split3(x)
@@ -42,7 +42,9 @@
     hi_t = jnp.where(xyz, hi, jnp.where(row == 3, 1.0, 0.0))
     mid_t = jnp.where(xyz, mid, 0.0)
     low_t = jnp.where(xyz, low, 0.0)
-    tgt[...] = jnp.concatenate([hi_t, hi_t, hi_t, mid_t, mid_t, low_t], 0).astype(jnp.bfloat16)
+    own = slice(HALO_T * TILE, (HALO_T + tiles) * TILE)
+    both = jnp.concatenate([hi_t, hi_t, hi_t, mid_t, mid_t, low_t], 0)[:, own]
+    tgt[...] = jnp.transpose(both.astype(jnp.bfloat16))
 
     def finish(n, slot):
         sums = [
@@ -53,13 +55,33 @@
         pull = jnp.concatenate([sums[1], sums[2], sums[3]], 0)
         out_ref[:, cols(n)] = fade * (own[:3] * sums[0] - pull)
 
+    def sources(n):
+        return [nb_ref[n + first, k] - first for k in range(NBR)]
+
+    def exponents(n, at):
+        lhs = tgt[cols(n), :]
+        both = [
+            jnp.concatenate([src[:, cols(at[k])], src[:, cols(at[k + 1])]], 1)
+            for k in range(0, NBR, 2)
+        ]
+        return [
+            jnp.dot(lhs, rhs, preferred_element_type=jnp.float32)
+            for rhs in both
+        ]
+
+    def prepare(n):
+        for k, part in enumerate(exponents(n, sources(n))):
+            expo[:, 2 * k * TILE : 2 * (k + 1) * TILE] = part
+
     def body(step, carry):
-        for s in range(UNROLL):
+        for s in range(UNROLL // 2, UNROLL):
             finish(jnp.maximum((step - 1) * UNROLL, 0) + s, s)
         for s in range(UNROLL):
+            if s == UNROLL // 2:
+                for done in range(s):
+                    finish(step * UNROLL + done, done)
             n = step * UNROLL + s
-            lhs = tgt[:, cols(n + HALO_T)]
-            at = [nb_ref[n + first, k] - first for k in range(NBR)]
+            at = sources(n)
             rows = [
                 [
                     jnp.broadcast_to(ext_ref[c : c + 1, cols(at[k] + first)], (8, TILE))
@@ -67,31 +89,30 @@
                 ]
                 for k in range(NBR)
             ]
-            expo = []
-            for k in range(0, NBR, 2):
-                rhs = jnp.concatenate([src[:, cols(at[k])], src[:, cols(at[k + 1])]], 1)
-                expo.append(
-                    lax.dot_general(
-                        lhs, rhs, (((0,), (0,)), ((), ())), preferred_element_type=jnp.float32
-                    )
-                )
+            parts = None if s == 0 else exponents(n, at)
             for g in range(0, TILE, 8):
                 total = None
                 for k in range(NBR):
                     half = (k % 2) * TILE
-                    u = jnp.exp2(expo[k // 2][g : g + 8, half : half + TILE])
-                    parts = [u, u * rows[k][0], u * rows[k][1], u * rows[k][2]]
-                    total = parts if k == 0 else [a + b for a, b in zip(total, parts)]
+                    if s == 0:
+                        e = expo[g : g + 8, k * TILE : (k + 1) * TILE]
+                    else:
+                        e = parts[k // 2][g : g + 8, half : half + TILE]
+                    u = jnp.exp2(e)
+                    add = [u, u * rows[k][0], u * rows[k][1], u * rows[k][2]]
+                    total = add if k == 0 else [a + b for a, b in zip(total, add)]
                 for c in range(4):
                     acc[s, c, g : g + 8, :] = total[c]
+        prepare(jnp.minimum((step + 1) * UNROLL, tiles - 1))
         return carry
 
     steps = tiles // UNROLL
     for s in range(UNROLL):
         for c in range(4):
             acc[s, c] = jnp.zeros((TILE, TILE), jnp.float32)
+    prepare(0)
     lax.fori_loop(0, steps, body, 0)
-    for s in range(UNROLL):
+    for s in range(UNROLL // 2, UNROLL):
         finish((steps - 1) * UNROLL + s, s)
 
 
@@ -109,8 +130,9 @@
         out_specs=pl.BlockSpec(memory_space=VMEM),
         scratch_shapes=[
             pltpu.VMEM((48, width), jnp.bfloat16),
-            pltpu.VMEM((48, width), jnp.bfloat16),
+            pltpu.VMEM((tiles * TILE, 48), jnp.bfloat16),
             pltpu.VMEM((UNROLL, 4, TILE, TILE), jnp.float32),
+            pltpu.VMEM((TILE, NBR * TILE), jnp.float32),
         ],
         cost_estimate=pl.CostEstimate(
             flops=pairs * 100, bytes_accessed=4 * 11 * width, transcendentals=pairs
@@ -202,55 +224,95 @@
     )(nb, *arrays, *after)
 
 
-def pack_kernel(order, pos_ref, out_ref):
-    size = out_ref.shape[2]
-    for b, share in enumerate(order):
-        out_ref[b] = pos_ref[:, share * size : (share + 1) * size]
-
-
-def pack(order, coords):
-    size = coords.shape[1] // len(order)
+def seat(order, odd, share):
+    there = order[len(order) - 1 - share]
+    return order[share] + odd * (there - order[share])
+
+
+def pack_kernel(order, odd_ref, pos_ref, charge_ref, out_ref, first_ref, last_ref):
+    size, rim, width = out_ref.shape[2], first_ref.shape[1], pos_ref.shape[2]
+    for share in range(len(order)):
+        b = seat(order, odd_ref[0], share)
+        for c in range(3):
+            out_ref[b, c : c + 1, :] = pos_ref[c, :, share * size : (share + 1) * size]
+    for ref, low in ((first_ref, 0), (last_ref, width - rim)):
+        for c in range(3):
+            ref[c : c + 1, :] = pos_ref[c, :, low : low + rim]
+        ref[3:4, :] = charge_ref[:, low : low + rim]
+
+
+def pack(order, rim, odd, coords, charges):
+    size = coords.shape[2] // len(order)
+    shapes = ((len(order), 3, size), (4, rim), (4, rim))
     return pl.pallas_call(
         functools.partial(pack_kernel, order),
-        out_shape=jax.ShapeDtypeStruct((len(order), 3, size), jnp.float32),
-        in_specs=[pl.BlockSpec(memory_space=VMEM)],
+        out_shape=[jax.ShapeDtypeStruct(shape, jnp.float32) for shape in shapes],
+        in_specs=[pl.BlockSpec(memory_space=SMEM)] + [pl.BlockSpec(memory_space=VMEM)] * 2,
+        out_specs=[pl.BlockSpec(memory_space=VMEM)] * 3,
+        compiler_params=pltpu.CompilerParams(vmem_limit_bytes=8 << 20),
+        name="pack",
+    )(odd, coords, charges)
+
+
+def extend_kernel(pos_ref, before_ref, after_ref, out_ref):
+    rim, width = before_ref.shape[1], pos_ref.shape[2]
+    out_ref[4:8, :] = jnp.zeros((4, width + 2 * rim), jnp.float32)
+    for at, size, rows in (
+        (0, rim, [before_ref[c : c + 1, :] for c in range(3)]),
+        (rim, width, [pos_ref[c] for c in range(3)]),
+        (rim + width, rim, [after_ref[c : c + 1, :] for c in range(3)]),
+    ):
+        rows = [math.sqrt(LOG2E) * x for x in rows]
+        for c in range(3):
+            out_ref[c : c + 1, at : at + size] = rows[c]
+        norm = rows[0] * rows[0] + rows[1] * rows[1] + rows[2] * rows[2]
+        out_ref[3:4, at : at + size] = -0.5 * norm
+
+
+def extend(pos, before, after):
+    width = pos.shape[2] + 2 * before.shape[1]
+    return pl.pallas_call(
+        extend_kernel,
+        out_shape=jax.ShapeDtypeStruct((8, width), jnp.float32),
+        in_specs=[pl.BlockSpec(memory_space=VMEM)] * 3,
         out_specs=pl.BlockSpec(memory_space=VMEM),
         compiler_params=pltpu.CompilerParams(vmem_limit_bytes=8 << 20),
-        name="pack",
-    )(coords)
-
-
-def total_kernel(order, plan, pos, last, following, masses, every, *refs):
-    short, out_ref = refs[:-1], refs[-1]
+        name="extend",
+    )(pos, before, after)
+
+
+def total_kernel(order, plan, odd_ref, pos, last, following, masses, every, dip, *refs):
+    short, (out_ref, dip_ref) = refs[:-2], refs[-2:]
     size = every.shape[2]
-    for b, share in enumerate(order):
+    dip_ref[...] = dip[...]
+    for share in range(len(order)):
         here = slice(share * size, (share + 1) * size)
         at, piece = share * size // TILE, 0
         while at >= plan[piece]:
             at, piece = at - plan[piece], piece + 1
-        spring = (SPRING * masses[:, here]) * (
-            last[:, here] + following[:, here] - 2.0 * pos[:, here]
-        )
-        force = short[piece][:, at * TILE : at * TILE + size] + spring + every[b]
-        for c in range(3):
-            out_ref[c, :, here] = force[c : c + 1]
-
-
-def total(order, plan, *arrays):
-    width = arrays[0].shape[1]
+        weight = SPRING * masses[:, here]
+        other = short[piece][:, at * TILE : at * TILE + size] + every[seat(order, odd_ref[0], share)]
+        for c in range(3):
+            pull = last[c, :, here] + following[c, :, here] - 2.0 * pos[c, :, here]
+            out_ref[c, :, here] = other[c : c + 1] + weight * pull
+
+
+def total(order, plan, odd, *arrays):
+    shapes = (arrays[0].shape, arrays[5].shape)
     return pl.pallas_call(
         functools.partial(total_kernel, order, plan),
-        out_shape=jax.ShapeDtypeStruct((3, 1, width), jnp.float32),
-        in_specs=[pl.BlockSpec(memory_space=VMEM)] * len(arrays),
-        out_specs=pl.BlockSpec(memory_space=VMEM),
+        out_shape=[jax.ShapeDtypeStruct(shape, jnp.float32) for shape in shapes],
+        in_specs=[pl.BlockSpec(memory_space=SMEM)]
+        + [pl.BlockSpec(memory_space=VMEM)] * len(arrays),
+        out_specs=[pl.BlockSpec(memory_space=VMEM)] * 2,
         compiler_params=pltpu.CompilerParams(vmem_limit_bytes=8 << 20),
         name="total",
-    )(*arrays)
+    )(odd, *arrays)
 
 
 def per_device(beads, spaces, positions, charges, polarizability, masses, neighbors):
-    coords = positions[0]
-    atom_dev = coords.shape[1]
+    coords = positions.transpose(1, 0, 2)
+    atom_dev = coords.shape[2]
     rim = HALO_T * TILE
     size = atom_dev // beads
     own_tiles = size // TILE
@@ -258,21 +320,26 @@
     across = math.gcd(beads, 8)
     bead = lax.axis_index("bead")
 
-    def share_of(b):
+    def fold(b):
         row, at = b // across, b % across
         return row * across + (across - 1 - at if row % 2 else at)
 
-    order = [share_of(b) for b in range(beads)]
+    order = [fold(b) for b in range(beads)]
     row, at = bead // across, bead % across
     share = row * across + jnp.where(row % 2 == 1, across - 1 - at, at)
+    odd = lax.axis_index("space") % 2
+    share = jnp.where(odd == 1, beads - 1 - share, share)
+    odd = odd.astype(jnp.int32).reshape(1)
     start = share * size
 
     def place(g):
-        return share_of(g % beads) * spaces + g // beads
+        domain = g // beads
+        return seat(order, domain % 2, g % beads) * spaces + domain
 
     count = beads * spaces
     fore = [(place(g), place((g + 1) % count)) for g in range(count)]
     back = [(j, i) for i, j in fore]
+    home = [(place(g), (g % beads) * spaces + g // beads) for g in range(count)]
     both = ("bead", "space")
 
     def around(x):
@@ -280,23 +347,20 @@
 
     up = [(s, (s + 1) % spaces) for s in range(spaces)]
     down = [(j, i) for i, j in up]
-    held = jnp.concatenate([coords, charges[None]], 0)
-    before = lax.ppermute(held[:, atom_dev - rim :], "space", up)
-    after = lax.ppermute(held[:, :rim], "space", down)
-    ext = jnp.concatenate([before, held, after], 1)
-    x = ext[:3] * math.sqrt(LOG2E)
-    ext8 = jnp.concatenate(
-        [x, -0.5 * jnp.sum(x * x, 0, keepdims=True), jnp.zeros((4, x.shape[1]), x.dtype)], 0
-    )
-    near_charge = lax.dynamic_slice(ext[3:4], (0, start), (1, size + 2 * rim))
-
-    shares = pack(order, coords)
+    charges = charges[None]
+    shares, first, final = pack(order, rim, odd, coords, charges)
+    before = lax.ppermute(final, "space", up)
+    after = lax.ppermute(first, "space", down)
+    ext8 = extend(coords, before, after)
+    near = jnp.concatenate([before[3:], charges, after[3:]], 1)
+    near_charge = lax.dynamic_slice(near, (0, start), (1, size + 2 * rim))
+
     cent = jnp.sum(lax.all_to_all(shares, "bead", 0, 0), axis=0) / beads
 
     own_rows = lax.dynamic_slice(neighbors, (share * own_tiles, 0), (own_tiles, NBR))
     nb = own_rows - share * own_tiles
     alpha = lax.dynamic_slice(polarizability, (start,), (size,))[None]
-    charge = lax.dynamic_slice(charges, (start,), (size,))[None]
+    charge = lax.dynamic_slice(charges, (0, start), (1, size))
 
     tiles = atom_dev // TILE
     plan = [n * tiles // sum(PLAN) for n in PLAN]
@@ -324,13 +388,14 @@
         hold = (fill(dip), last, following) if sweep == 1 else (fill(dip),)
         dip = centre("dipole", beads, hold, nb, *c3, *d3, alpha, state)
     d3 = around(dip)
-    pulled = centre("pulled", beads, (fill(dip),), nb, *c3, *d3, charge)
+    dipoles = lax.ppermute(dip, both, home)
+    pulled = centre("pulled", beads, (fill(dip), dipoles), nb, *c3, *d3, charge)
     fill(pulled)
     every = lax.all_to_all(pulled, "bead", 0, 0)
-    forces = total(order, plan, coords, last, following, masses[None], every, *short)
-    forces = forces.transpose(1, 0, 2)
-    dipoles = lax.ppermute(dip, "bead", [(b, share_of(b)) for b in range(beads)])
-    return forces, dipoles
+    forces, dipoles = total(
+        order, plan, odd, coords, last, following, masses[None], every, dipoles, *short
+    )
+    return forces.transpose(1, 0, 2), dipoles
 
 
 def solution(mesh):

time: 118 us -> 110 us (0.932)
  the two profiles are of different devices: /device:TPU:40 before, /device:TPU:6 now
where the time goes in v2:
time: 110 us
  Pallas kernels  57.9 us (53%)
  starting transfers between devices  42.3 us (38%)
  waiting for transfers between devices  5.1 us (5%)
  local copies, waits for them, and re-layouts  3.41 us (3%)
    pallas_call x7, Pallas kernels, short_range(): pl.pallas_call(functools.partial(short_kernel, tiles, first), out_shape=j...  40.8 us
    pallas_call x5, Pallas kernels, centre(): pl.pallas_call(functools.partial(centre_kernel, mode, size // TILE), out_...  15.4 us
    ppermute x10, starting transfers between devices, around(): return (lax.ppermute(x, both, fore), x, lax.ppermute(x, both, back))  13.7 us
    all_to_all x1, starting transfers between devices, per_device(): cent = jnp.sum(lax.all_to_all(shares, 'bead', 0, 0), axis=0) / beads  11.6 us
    all_to_all x1, starting transfers between devices, per_device(): every = lax.all_to_all(pulled, 'bead', 0, 0)  10.5 us
    ppermute x1, starting transfers between devices, per_device(): following = lax.ppermute(late, 'bead', turn_back)  4.07 us
    all_to_all x1, waiting for transfers between devices, per_device(): every = lax.all_to_all(pulled, 'bead', 0, 0)  3.84 us
    unnamed x13, local copies, waits for them, and re-layouts  2.56 us
  transfers between devices with their start and end apart: 17, of which 2 were waited for; matrix products, arithmetic and copies ran while one was open for 1% of the time, Pallas kernels for 40%

profile of v2, /device:TPU:6, one launch (start us, length us, event | category | flops | bytes accessed | tf_op | source)
XLA Modules:
  0.0 109.8 jit_solution(9400881648179935174)
XLA Ops:
  0.7 0.9 copy-done
  1.6 0.8 copy-done.2
  2.4 0.8 pack.1
  3.2 11.6 %all-to-all-start = ((f32[32,3,512]{2,1,0:T(4,128)}), f32[32,3,512]{2,1,0:T(4,128)S(1)}, u32[]{:S(2)}, u32[]{:S(2)}) async-start(f32[32,3,512]{2,1,0:T(4,128)} %get-tuple-element.10.after_ref), calls=%async_computation | async-start | bytes 524288 | tf_op jit(solution)/shard_map/all_to_all | solution.py:358
  14.8 1.7 %collective-permute-start.1 = (f32[4,512]{1,0:T(4,128)S(1)}, f32[4,512]{1,0:T(4,128)S(1)}, u32[]{:S(2)}, u32[]{:S(2)}) collective-permute-start(f32[4,512]{1,0:T(4,128)S(1)} %get-tuple-element.12), channel_id=1, source_target_pairs={{1,0},{2,1},{3,2},{4,3},{5,4},{6,5},{7,6},{0,7},{9,8},{10,9},{11,1... | collective-permute-start | bytes 24584 | tf_op jit(solution)/shard_map/ppermute | solution.py:353
  16.6 0.7 copy-done.5
  17.4 0.8 dynamic_slice.14
  18.3 7.7 %short_range.7.refs_0_ = f32[3,3584]{1,0:T(4,128)S(1)} custom-call(s32[128,8]{1,0:T(8,128)S(1)} %copy.7.nb_ref, f32[8,17408]{1,0:T(8,128)S(1)} %extend.1.ext_ref, f32[32,3,512]{2,1,0:T(4,128)} %get-tuple-element.10.after_ref), custom_call_target="tpu_custom_call" | custom-call | flops 367001600 | bytes 202752 | tf_op jit(solution)/shard_map/short_range/pallas_call | solution.py:122
  26.0 1.2 %all-to-all-done = f32[32,3,512]{2,1,0:T(4,128)S(1)} async-done(((f32[32,3,512]{2,1,0:T(4,128)}), f32[32,3,512]{2,1,0:T(4,128)S(1)}, u32[]{:S(2)}, u32[]{:S(2)}) %all-to-all-start) | async-done | bytes 196640 | tf_op jit(solution)/shard_map/all_to_all | solution.py:358
  27.9 1.5 %collective-permute-start.2 = (f32[3,512]{1,0:T(4,128)S(1)}, f32[3,512]{1,0:T(4,128)S(1)}, u32[]{:S(2)}, u32[]{:S(2)}) collective-permute-start(f32[3,512]{1,0:T(4,128)S(1)} %broadcast_multiply_fusion.after_ref.refs_1_), channel_id=1, source_target_pairs={{0,8},{8,16},{16,24},{24,32},{32,40},{40,48},{48,56},{56,120},{120... | collective-permute-start | bytes 18440 | tf_op jit(solution)/shard_map/ppermute | solution.py:346
  29.4 4.5 %short_range.8.refs_5_.refs_1_ = f32[3,1536]{1,0:T(4,128)S(1)} custom-call(s32[128,8]{1,0:T(8,128)S(1)} %copy.7.nb_ref, f32[8,17408]{1,0:T(8,128)S(1)} %extend.1.ext_ref, f32[3,512]{1,0:T(4,128)S(1)} %broadcast_multiply_fusion.after_ref.refs_1_), custom_call_target="tpu_custom_call" | custom-call | flops 157286400 | bytes 112640 | tf_op jit(solution)/shard_map/short_range/pallas_call | solution.py:122
  33.9 2.1 %shard_map.68.refs_7_ = f32[6,512]{1,0:T(8,128)S(1)} custom-call(s32[4,8]{1,0:T(4,128)S(1)} %dynamic-slice_subtract_fusion.nb_ref, f32[3,512]{1,0:T(4,128)S(1)} %collective-permute-done.2.refs_0_, f32[3,512]{1,0:T(4,128)S(1)} %broadcast_multiply_fusion.after_ref.refs_1_, f32[3,512]{1,0:T(4,128)S(1)} %collective-permute-done.3.refs_2_, ...), custom_call_target="tpu_custom_call" | custom-call | flops 52428800 | bytes 49152 | tf_op jit(solution)/shard_map/pallas_call | solution.py:208
  36.1 4.1 %collective-permute-start.5 = (f32[3,1,16384]{2,1,0:T(1,128)S(1)}, f32[3,1,16384]{2,1,0:T(1,128)S(1)}, u32[]{:S(2)}, u32[]{:S(2)}) collective-permute-start(f32[3,1,16384]{2,1,0:T(1,128)S(1)} %bitcast.9), channel_id=1, source_target_pairs={{8,0},{16,8},{24,16},{32,24},{40,32},{48,40},{56,48},{64,56},{72,6... | collective-permute-start | bytes 589832 | tf_op jit(solution)/shard_map/ppermute | solution.py:384
  40.2 0.9 collective-permute-start.7
  41.2 1.1 %collective-permute-start.6 = (f32[3,512]{1,0:T(4,128)S(1)}, f32[3,512]{1,0:T(4,128)S(1)}, u32[]{:S(2)}, u32[]{:S(2)}) collective-permute-start(f32[3,512]{1,0:T(4,128)S(1)} %slice.11.after_ref.refs_4_), channel_id=1, source_target_pairs={{0,8},{8,16},{16,24},{24,32},{32,40},{40,48},{48,56},{56,120},{120... | collective-permute-start | bytes 18440 | tf_op jit(solution)/shard_map/ppermute | solution.py:346
  42.3 5.4 %short_range.9.refs_8_.refs_2_ = f32[3,2048]{1,0:T(4,128)S(1)} custom-call(s32[128,8]{1,0:T(8,128)S(1)} %copy.7.nb_ref, f32[8,17408]{1,0:T(8,128)S(1)} %extend.1.ext_ref, f32[3,512]{1,0:T(4,128)S(1)} %slice.11.after_ref.refs_4_), custom_call_target="tpu_custom_call" | custom-call | flops 209715200 | bytes 135168 | tf_op jit(solution)/shard_map/short_range/pallas_call | solution.py:122
  47.7 3.1 %shard_map.69.after_ref.refs_4_ = f32[3,512]{1,0:T(4,128)S(1)} custom-call(s32[4,8]{1,0:T(4,128)S(1)} %dynamic-slice_subtract_fusion.nb_ref, f32[3,512]{1,0:T(4,128)S(1)} %collective-permute-done.2.refs_0_, f32[3,512]{1,0:T(4,128)S(1)} %broadcast_multiply_fusion.after_ref.refs_1_, f32[3,512]{1,0:T(4,128)S(1)} %collective-permute-done.3.refs_2_, ...), custom_call_target="tpu_custom_call" | custom-call | flops 52428800 | bytes 49152 | tf_op jit(solution)/shard_map/pallas_call | solution.py:208
  50.9 0.7 collective-permute-start.9
  51.6 1.4 %collective-permute-start.8 = (f32[3,512]{1,0:T(4,128)S(1)}, f32[3,512]{1,0:T(4,128)S(1)}, u32[]{:S(2)}, u32[]{:S(2)}) collective-permute-start(f32[3,512]{1,0:T(4,128)S(1)} %shard_map.69.after_ref.refs_4_), channel_id=1, source_target_pairs={{0,8},{8,16},{16,24},{24,32},{32,40},{40,48},{48,56},{56,120},{120... | collective-permute-start | bytes 18440 | tf_op jit(solution)/shard_map/ppermute | solution.py:346
  53.0 4.5 %short_range.10.refs_8_.refs_3_ = f32[3,1536]{1,0:T(4,128)S(1)} custom-call(s32[128,8]{1,0:T(8,128)S(1)} %copy.7.nb_ref, f32[8,17408]{1,0:T(8,128)S(1)} %extend.1.ext_ref, f32[3,512]{1,0:T(4,128)S(1)} %shard_map.69.after_ref.refs_4_), custom_call_target="tpu_custom_call" | custom-call | flops 157286400 | bytes 112640 | tf_op jit(solution)/shard_map/short_range/pallas_call | solution.py:122
  57.5 3.1 %shard_map.70.after_ref.refs_4_ = f32[3,512]{1,0:T(4,128)S(1)} custom-call(s32[4,8]{1,0:T(4,128)S(1)} %dynamic-slice_subtract_fusion.nb_ref, f32[3,512]{1,0:T(4,128)S(1)} %collective-permute-done.2.refs_0_, f32[3,512]{1,0:T(4,128)S(1)} %broadcast_multiply_fusion.after_ref.refs_1_, f32[3,512]{1,0:T(4,128)S(1)} %collective-permute-done.3.refs_2_, ...), custom_call_target="tpu_custom_call" | custom-call | flops 52428800 | bytes 49152 | tf_op jit(solution)/shard_map/pallas_call | solution.py:208
  61.1 1.7 %collective-permute-start.10 = (f32[3,512]{1,0:T(4,128)S(1)}, f32[3,512]{1,0:T(4,128)S(1)}, u32[]{:S(2)}, u32[]{:S(2)}) collective-permute-start(f32[3,512]{1,0:T(4,128)S(1)} %shard_map.70.after_ref.refs_4_), channel_id=1, source_target_pairs={{0,8},{8,16},{16,24},{24,32},{32,40},{40,48},{48,56},{56,120},{120... | collective-permute-start | bytes 18440 | tf_op jit(solution)/shard_map/ppermute | solution.py:346
  62.7 5.4 %short_range.11.refs_8_.refs_4_ = f32[3,2048]{1,0:T(4,128)S(1)} custom-call(s32[128,8]{1,0:T(8,128)S(1)} %copy.7.nb_ref, f32[8,17408]{1,0:T(8,128)S(1)} %extend.1.ext_ref, f32[3,512]{1,0:T(4,128)S(1)} %shard_map.70.after_ref.refs_4_), custom_call_target="tpu_custom_call" | custom-call | flops 209715200 | bytes 135168 | tf_op jit(solution)/shard_map/short_range/pallas_call | solution.py:122
  68.2 3.1 %shard_map.71.after_ref.refs_4_ = f32[3,512]{1,0:T(4,128)S(1)} custom-call(s32[4,8]{1,0:T(4,128)S(1)} %dynamic-slice_subtract_fusion.nb_ref, f32[3,512]{1,0:T(4,128)S(1)} %collective-permute-done.2.refs_0_, f32[3,512]{1,0:T(4,128)S(1)} %broadcast_multiply_fusion.after_ref.refs_1_, f32[3,512]{1,0:T(4,128)S(1)} %collective-permute-done.3.refs_2_, ...), custom_call_target="tpu_custom_call" | custom-call | flops 52428800 | bytes 49152 | tf_op jit(solution)/shard_map/pallas_call | solution.py:208
  71.3 0.7 collective-permute-start.14
  72.0 5.3 %collective-permute-start.13 = (f32[3,512]{1,0:T(4,128)S(1)}, f32[3,512]{1,0:T(4,128)S(1)}, u32[]{:S(2)}, u32[]{:S(2)}) collective-permute-start(f32[3,512]{1,0:T(4,128)S(1)} %shard_map.71.after_ref.refs_4_), channel_id=1, source_target_pairs={{8,0},{16,8},{24,16},{32,24},{40,32},{48,40},{56,48},{120,56},{112... | collective-permute-start | bytes 18440 | tf_op jit(solution)/shard_map/ppermute | solution.py:346
  77.3 4.5 %short_range.12.refs_7_.refs_5_ = f32[3,1536]{1,0:T(4,128)S(1)} custom-call(s32[128,8]{1,0:T(8,128)S(1)} %copy.7.nb_ref, f32[8,17408]{1,0:T(8,128)S(1)} %extend.1.ext_ref, f32[3,512]{1,0:T(4,128)S(1)} %shard_map.71.after_ref.refs_4_), custom_call_target="tpu_custom_call" | custom-call | flops 157286400 | bytes 112640 | tf_op jit(solution)/shard_map/short_range/pallas_call | solution.py:122
  81.8 3.9 %shard_map.72.after_ref = f32[32,3,512]{2,1,0:T(4,128)} custom-call(s32[4,8]{1,0:T(4,128)S(1)} %dynamic-slice_subtract_fusion.nb_ref, f32[3,512]{1,0:T(4,128)S(1)} %collective-permute-done.2.refs_0_, f32[3,512]{1,0:T(4,128)S(1)} %broadcast_multiply_fusion.after_ref.refs_1_, f32[3,512]{1,0:T(4,128)S(1)} %collective-permute-done.3.refs_2_, ...), custom_call_target="tpu_custom_call" | custom-call | flops 52428800 | bytes 49152 | tf_op jit(solution)/shard_map/pallas_call | solution.py:208
  85.7 10.5 %all-to-all-start.1 = ((f32[32,3,512]{2,1,0:T(4,128)}), f32[32,3,512]{2,1,0:T(4,128)S(1)}, u32[]{:S(2)}, u32[]{:S(2)}) async-start(f32[32,3,512]{2,1,0:T(4,128)} %shard_map.72.after_ref), calls=%async_computation.1 | async-start | bytes 524288 | tf_op jit(solution)/shard_map/all_to_all | solution.py:394
  96.2 8.9 %short_range.13.refs_6_ = f32[3,4096]{1,0:T(4,128)S(1)} custom-call(s32[128,8]{1,0:T(8,128)S(1)} %copy.7.nb_ref, f32[8,17408]{1,0:T(8,128)S(1)} %extend.1.ext_ref, f32[32,3,512]{2,1,0:T(4,128)} %shard_map.72.after_ref), custom_call_target="tpu_custom_call" | custom-call | flops 419430400 | bytes 225280 | tf_op jit(solution)/shard_map/short_range/pallas_call | solution.py:122
  105.1 3.8 %all-to-all-done.1.every = f32[32,3,512]{2,1,0:T(4,128)S(1)} async-done(((f32[32,3,512]{2,1,0:T(4,128)}), f32[32,3,512]{2,1,0:T(4,128)S(1)}, u32[]{:S(2)}, u32[]{:S(2)}) %all-to-all-start.1) | async-done | bytes 196640 | tf_op jit(solution)/shard_map/all_to_all | solution.py:394
  108.9 0.9 total.1
  (39 shorter events, 1.6 us)
Async XLA Ops:
  0.6 0.9 copy-start
  1.6 0.8 copy-start.2
  3.2 15.0 %copy-start.1 = (f32[1,3,16384]{2,0,1:T(1,128)S(1)}, f32[1,3,16384]{2,0,1:T(1,128)}, u32[]{:S(2)}) copy-start(f32[1,3,16384]{2,0,1:T(1,128)} %param.5) | copy-start | bytes 589828
  3.2 24.1 %all-to-all-start = ((f32[32,3,512]{2,1,0:T(4,128)}), f32[32,3,512]{2,1,0:T(4,128)S(1)}, u32[]{:S(2)}, u32[]{:S(2)}) async-start(f32[32,3,512]{2,1,0:T(4,128)} %get-tuple-element.10.after_ref), calls=%async_computation | async-start | bytes 524288 | tf_op jit(solution)/shard_map/all_to_all | solution.py:358
  14.8 3.3 %collective-permute-start = (f32[4,512]{1,0:T(4,128)S(1)}, f32[4,512]{1,0:T(4,128)S(1)}, u32[]{:S(2)}, u32[]{:S(2)}) collective-permute-start(f32[4,512]{1,0:T(4,128)S(1)} %get-tuple-element.11), channel_id=1, source_target_pairs={{0,1},{1,2},{2,3},{3,4},{4,5},{5,6},{6,7},{7,0},{8,9},{9,10},{10,1... | collective-permute-start | bytes 24584 | tf_op jit(solution)/shard_map/ppermute | solution.py:352
  14.8 3.3 %collective-permute-start.1 = (f32[4,512]{1,0:T(4,128)S(1)}, f32[4,512]{1,0:T(4,128)S(1)}, u32[]{:S(2)}, u32[]{:S(2)}) collective-permute-start(f32[4,512]{1,0:T(4,128)S(1)} %get-tuple-element.12), channel_id=1, source_target_pairs={{1,0},{2,1},{3,2},{4,3},{5,4},{6,5},{7,6},{0,7},{9,8},{10,9},{11,1... | collective-permute-start | bytes 24584 | tf_op jit(solution)/shard_map/ppermute | solution.py:353
  16.6 0.7 copy-start.5
  18.3 7.7 %copy-start.3 = (f32[16384]{0:T(1024)S(1)}, f32[16384]{0:T(1024)}, u32[]{:S(2)}) copy-start(f32[16384]{0:T(1024)} %param.6) | copy-start | bytes 196612
  27.3 6.6 %collective-permute-start.3 = (f32[3,512]{1,0:T(4,128)S(1)}, f32[3,512]{1,0:T(4,128)S(1)}, u32[]{:S(2)}, u32[]{:S(2)}) collective-permute-start(f32[3,512]{1,0:T(4,128)S(1)} %broadcast_multiply_fusion.after_ref.refs_1_), channel_id=1, source_target_pairs={{8,0},{16,8},{24,16},{32,24},{40,32},{48,40},{56,48},{120,56},{112... | collective-permute-start | bytes 18440 | tf_op jit(solution)/shard_map/ppermute | solution.py:346
  27.9 6.0 %collective-permute-start.2 = (f32[3,512]{1,0:T(4,128)S(1)}, f32[3,512]{1,0:T(4,128)S(1)}, u32[]{:S(2)}, u32[]{:S(2)}) collective-permute-start(f32[3,512]{1,0:T(4,128)S(1)} %broadcast_multiply_fusion.after_ref.refs_1_), channel_id=1, source_target_pairs={{0,8},{8,16},{16,24},{24,32},{32,40},{40,48},{48,56},{56,120},{120... | collective-permute-start | bytes 18440 | tf_op jit(solution)/shard_map/ppermute | solution.py:346
  36.1 21.4 %collective-permute-start.5 = (f32[3,1,16384]{2,1,0:T(1,128)S(1)}, f32[3,1,16384]{2,1,0:T(1,128)S(1)}, u32[]{:S(2)}, u32[]{:S(2)}) collective-permute-start(f32[3,1,16384]{2,1,0:T(1,128)S(1)} %bitcast.9), channel_id=1, source_target_pairs={{8,0},{16,8},{24,16},{32,24},{40,32},{48,40},{56,48},{64,56},{72,6... | collective-permute-start | bytes 589832 | tf_op jit(solution)/shard_map/ppermute | solution.py:384
  40.1 17.3 %collective-permute-start.4 = (f32[3,1,16384]{2,1,0:T(1,128)S(1)}, f32[3,1,16384]{2,1,0:T(1,128)S(1)}, u32[]{:S(2)}, u32[]{:S(2)}) collective-permute-start(f32[3,1,16384]{2,1,0:T(1,128)S(1)} %bitcast.10), channel_id=1, source_target_pairs={{0,8},{8,16},{16,24},{24,32},{32,40},{40,48},{48,56},{56,64},{64,7... | collective-permute-start | bytes 589832 | tf_op jit(solution)/shard_map/ppermute | solution.py:383
  40.2 7.5 %collective-permute-start.7 = (f32[3,512]{1,0:T(4,128)S(1)}, f32[3,512]{1,0:T(4,128)S(1)}, u32[]{:S(2)}, u32[]{:S(2)}) collective-permute-start(f32[3,512]{1,0:T(4,128)S(1)} %slice.11.after_ref.refs_4_), channel_id=1, source_target_pairs={{8,0},{16,8},{24,16},{32,24},{40,32},{48,40},{56,48},{120,56},{112... | collective-permute-start | bytes 18440 | tf_op jit(solution)/shard_map/ppermute | solution.py:346
  41.2 6.6 %collective-permute-start.6 = (f32[3,512]{1,0:T(4,128)S(1)}, f32[3,512]{1,0:T(4,128)S(1)}, u32[]{:S(2)}, u32[]{:S(2)}) collective-permute-start(f32[3,512]{1,0:T(4,128)S(1)} %slice.11.after_ref.refs_4_), channel_id=1, source_target_pairs={{0,8},{8,16},{16,24},{24,32},{32,40},{40,48},{48,56},{56,120},{120... | collective-permute-start | bytes 18440 | tf_op jit(solution)/shard_map/ppermute | solution.py:346
  50.9 6.6 %collective-permute-start.9 = (f32[3,512]{1,0:T(4,128)S(1)}, f32[3,512]{1,0:T(4,128)S(1)}, u32[]{:S(2)}, u32[]{:S(2)}) collective-permute-start(f32[3,512]{1,0:T(4,128)S(1)} %shard_map.69.after_ref.refs_4_), channel_id=1, source_target_pairs={{8,0},{16,8},{24,16},{32,24},{40,32},{48,40},{56,48},{120,56},{112... | collective-permute-start | bytes 18440 | tf_op jit(solution)/shard_map/ppermute | solution.py:346
  51.6 5.9 %collective-permute-start.8 = (f32[3,512]{1,0:T(4,128)S(1)}, f32[3,512]{1,0:T(4,128)S(1)}, u32[]{:S(2)}, u32[]{:S(2)}) collective-permute-start(f32[3,512]{1,0:T(4,128)S(1)} %shard_map.69.after_ref.refs_4_), channel_id=1, source_target_pairs={{0,8},{8,16},{16,24},{24,32},{32,40},{40,48},{48,56},{56,120},{120... | collective-permute-start | bytes 18440 | tf_op jit(solution)/shard_map/ppermute | solution.py:346
  60.6 7.5 %collective-permute-start.11 = (f32[3,512]{1,0:T(4,128)S(1)}, f32[3,512]{1,0:T(4,128)S(1)}, u32[]{:S(2)}, u32[]{:S(2)}) collective-permute-start(f32[3,512]{1,0:T(4,128)S(1)} %shard_map.70.after_ref.refs_4_), channel_id=1, source_target_pairs={{8,0},{16,8},{24,16},{32,24},{40,32},{48,40},{56,48},{120,56},{112... | collective-permute-start | bytes 18440 | tf_op jit(solution)/shard_map/ppermute | solution.py:346
  61.1 7.1 %collective-permute-start.10 = (f32[3,512]{1,0:T(4,128)S(1)}, f32[3,512]{1,0:T(4,128)S(1)}, u32[]{:S(2)}, u32[]{:S(2)}) collective-permute-start(f32[3,512]{1,0:T(4,128)S(1)} %shard_map.70.after_ref.refs_4_), channel_id=1, source_target_pairs={{0,8},{8,16},{16,24},{24,32},{32,40},{40,48},{48,56},{56,120},{120... | collective-permute-start | bytes 18440 | tf_op jit(solution)/shard_map/ppermute | solution.py:346
  71.3 10.4 %collective-permute-start.14 = (f32[3,512]{1,0:T(4,128)S(1)}, f32[3,512]{1,0:T(4,128)S(1)}, u32[]{:S(2)}, u32[]{:S(2)}) collective-permute-start(f32[3,512]{1,0:T(4,128)S(1)} %shard_map.71.after_ref.refs_4_), channel_id=1, source_target_pairs={{0,0},{8,8},{16,16},{24,24},{32,32},{40,40},{48,48},{56,56},{120,6... | collective-permute-start | bytes 18440 | tf_op jit(solution)/shard_map/ppermute | solution.py:391
  72.0 9.8 %collective-permute-start.13 = (f32[3,512]{1,0:T(4,128)S(1)}, f32[3,512]{1,0:T(4,128)S(1)}, u32[]{:S(2)}, u32[]{:S(2)}) collective-permute-start(f32[3,512]{1,0:T(4,128)S(1)} %shard_map.71.after_ref.refs_4_), channel_id=1, source_target_pairs={{8,0},{16,8},{24,16},{32,24},{40,32},{48,40},{56,48},{120,56},{112... | collective-permute-start | bytes 18440 | tf_op jit(solution)/shard_map/ppermute | solution.py:346
  77.3 4.5 %collective-permute-start.12 = (f32[3,512]{1,0:T(4,128)S(1)}, f32[3,512]{1,0:T(4,128)S(1)}, u32[]{:S(2)}, u32[]{:S(2)}) collective-permute-start(f32[3,512]{1,0:T(4,128)S(1)} %shard_map.71.after_ref.refs_4_), channel_id=1, source_target_pairs={{0,8},{8,16},{16,24},{24,32},{32,40},{40,48},{48,56},{56,120},{120... | collective-permute-start | bytes 18440 | tf_op jit(solution)/shard_map/ppermute | solution.py:346
  85.7 23.2 %all-to-all-start.1 = ((f32[32,3,512]{2,1,0:T(4,128)}), f32[32,3,512]{2,1,0:T(4,128)S(1)}, u32[]{:S(2)}, u32[]{:S(2)}) async-start(f32[32,3,512]{2,1,0:T(4,128)} %shard_map.72.after_ref), calls=%async_computation.1 | async-start | bytes 524288 | tf_op jit(solution)/shard_map/all_to_all | solution.py:394
  96.2 12.7 %copy-start.4 = (f32[16384]{0:T(1024)S(1)}, f32[16384]{0:T(1024)}, u32[]{:S(2)}) copy-start(f32[16384]{0:T(1024)} %param.8) | copy-start | bytes 196612

commit v3 on v2

--- a/solution.py
+++ b/solution.py
@@ -16,7 +16,7 @@
 REPULSION = 0.2
 SPRING = 0.1
 UNROLL = 4
-PLAN = (28, 12, 16, 12, 16, 12, 32)
+PLAN = (36, 16, 16, 16, 16, 16, 12)
 VMEM = pltpu.MemorySpace.VMEM
 SMEM = pltpu.MemorySpace.SMEM
 
@@ -56,7 +56,7 @@
         out_ref[:, cols(n)] = fade * (own[:3] * sums[0] - pull)
 
     def sources(n):
-        return [nb_ref[n + first, k] - first for k in range(NBR)]
+        return [nb_ref[k, n + first] - first for k in range(NBR)]
 
     def exponents(n, at):
         lhs = tgt[cols(n), :]
@@ -107,9 +107,6 @@
         return carry
 
     steps = tiles // UNROLL
-    for s in range(UNROLL):
-        for c in range(4):
-            acc[s, c] = jnp.zeros((TILE, TILE), jnp.float32)
     prepare(0)
     lax.fori_loop(0, steps, body, 0)
     for s in range(UNROLL // 2, UNROLL):
@@ -142,86 +139,128 @@
     )(neighbors, ext8, after)
 
 
-def centre_kernel(mode, own_tiles, nb_ref, *refs):
-    ins, (out_ref, win, spread, acc) = refs, refs[-4:]
+def rows16(x):
+    hi, mid, low = split3(x)
+    return jnp.concatenate([hi, mid, low], 0).astype(jnp.bfloat16)
+
+
+def contract(high, rest, feats):
+    dims = (((1,), (1,)), ((), ()))
+    out = lax.dot_general(high, feats, dims, preferred_element_type=jnp.float32)
+    out += lax.dot_general(rest, feats, dims, preferred_element_type=jnp.float32)
+    out = jnp.transpose(out)
+    return out[:16] + out[16:32] + out[32:48]
+
+
+def gather(ref, nb_ref, t):
+    return jnp.concatenate([ref[:, cols(nb_ref[t, k])] for k in range(NBR)], 1)
+
+
+def fade_of(x):
+    return jnp.exp2((-0.25 * LOG2E) * jnp.sum(x * x, axis=0, keepdims=True))
+
+
+def first_kernel(own_tiles, nb_ref, before, own, after, charge, alpha, *refs):
+    out_ref, high_ref, rest_ref, win, src, tgt, feats = refs[-7:]
     size = own_tiles * TILE
-    if mode == "permanent":
-        before, own, after, charge, alpha = ins[:5]
-    else:
-        before, own, after, dip_b, dip_o, dip_a, scale = ins[:7]
-    parts = (before, own, after)
-    for p in range(3):
-        win[0:3, p * size : (p + 1) * size] = parts[p][...]
-    if mode == "permanent":
-        win[3:4, :] = charge[...]
-    else:
-        for p, dip in enumerate((dip_b, dip_o, dip_a)):
-            win[3:6, p * size : (p + 1) * size] = dip[0:3, :]
-
-    def body(t):
-        for c in range(3):
-            line = win[c : c + 1, (t + HALO_T) * TILE : (t + HALO_T + 1) * TILE]
-            spread[t, c] = jnp.transpose(jnp.broadcast_to(line, (TILE, TILE)))
-        at = [nb_ref[t, k] for k in range(NBR)]
-        wide = 4 if mode == "permanent" else 6
-        rows = [
-            [jnp.broadcast_to(win[c : c + 1, cols(at[k])], (8, TILE)) for c in range(wide)]
-            for k in range(NBR)
+    for p, part in enumerate((before, own, after)):
+        win[0:3, p * size : (p + 1) * size] = part[...]
+    x = win[0:3, :]
+    q = charge[...]
+    y = math.sqrt(0.5 * LOG2E) * x
+    norm = -0.5 * jnp.sum(y * y, axis=0, keepdims=True)
+    zero = jnp.zeros((4, 3 * size), jnp.float32)
+    hi, mid, low = split3(jnp.concatenate([y, norm, zero], 0))
+    src[...] = jnp.concatenate([hi, mid, low, hi, mid, hi], 0).astype(jnp.bfloat16)
+    row = lax.broadcasted_iota(jnp.int32, hi.shape, 0)
+    hi_t = jnp.where(row < 3, hi, jnp.where(row == 3, 1.0, 0.0))
+    mid_t, low_t = jnp.where(row < 3, mid, 0.0), jnp.where(row < 3, low, 0.0)
+    both = jnp.concatenate([hi_t, hi_t, hi_t, mid_t, mid_t, low_t], 0)[:, size : 2 * size]
+    tgt[...] = jnp.transpose(both.astype(jnp.bfloat16))
+    feats[...] = rows16(jnp.concatenate([q, q * x, zero, zero, zero], 0))
+    for t in range(own_tiles):
+        here = slice(t * TILE, (t + 1) * TILE)
+        e = jnp.dot(tgt[here, :], gather(src, nb_ref, t), preferred_element_type=jnp.float32)
+        u = jnp.exp2(e)
+        high = u.astype(jnp.bfloat16)
+        rest = (u - high.astype(jnp.float32)).astype(jnp.bfloat16)
+        high_ref[here, :] = high
+        rest_ref[here, :] = rest
+        sums = contract(high, rest, gather(feats, nb_ref, t))
+        me = own[:, here]
+        field = fade_of(me) * (me * sums[0:1] - sums[1:4])
+        out_ref[0:3, here] = alpha[:, here] * field
+        out_ref[3:6, here] = field
+
+
+def next_kernel(last, own_tiles, nb_ref, before, own, after, dip_b, dip_o, dip_a, *refs):
+    scale, state, high_ref, rest_ref = refs[:4]
+    out_ref, feats = refs[-2:]
+    size = own_tiles * TILE
+    parts = ((before, dip_b), (own, dip_o), (after, dip_a))
+    for p, (place, dip) in enumerate(parts):
+        x, m = place[...], dip[0:3, :]
+        along = jnp.sum(x * m, axis=0, keepdims=True)
+        rows = [m, along, x[0:1] * m, x[1:2] * m, x[2:3] * m, x * along]
+        feats[:, p * size : (p + 1) * size] = rows16(jnp.concatenate(rows, 0))
+    for t in range(own_tiles):
+        here = slice(t * TILE, (t + 1) * TILE)
+        sums = contract(high_ref[here, :], rest_ref[here, :], gather(feats, nb_ref, t))
+        me = own[:, here]
+        ahead = jnp.sum(me * sums[0:3], axis=0, keepdims=True) - sums[3:4]
+        turned = [
+            jnp.sum(me * sums[4 + 3 * c : 7 + 3 * c], axis=0, keepdims=True) for c in range(3)
         ]
-        for g in range(0, TILE, 8):
-            me = [spread[t, c, g : g + 8, :] for c in range(3)]
-            total = None
-            for k in range(NBR):
-                d = [me[c] - rows[k][c] for c in range(3)]
-                r2 = d[0] * d[0] + d[1] * d[1] + d[2] * d[2]
-                w = jnp.exp2((-0.25 * LOG2E) * r2)
-                if mode == "permanent":
-                    w = w * rows[k][3]
-                    add = [w * d[c] for c in range(3)]
-                else:
-                    m = rows[k][3:6]
-                    p = 0.25 * (d[0] * m[0] + d[1] * m[1] + d[2] * m[2])
-                    add = [w * (p * d[c] - 0.5 * m[c]) for c in range(3)]
-                total = add if k == 0 else [a + b for a, b in zip(total, add)]
-            for c in range(3):
-                acc[t, c, g : g + 8, :] = total[c]
-        here = slice(t * TILE, (t + 1) * TILE)
-        for c in range(3):
-            s = jnp.sum(jnp.transpose(acc[t, c]), axis=0, keepdims=True)
-            if mode == "permanent":
-                out_ref[c : c + 1, here] = alpha[:, here] * s
-                out_ref[3 + c : 4 + c, here] = s
-            elif mode == "dipole":
-                out_ref[c : c + 1, here] = scale[:, here] * (ins[7][3 + c : 4 + c, here] + s)
-            else:
-                line = scale[:, here] * s
-                out_ref[:, c : c + 1, here] = jnp.broadcast_to(line, (out_ref.shape[0], 1, TILE))
-
-    for t in range(own_tiles):
-        body(t)
-
-
-def centre(mode, copies, after, nb, *arrays):
+        pull = me * ahead - jnp.concatenate(turned, 0) + sums[13:16]
+        field = fade_of(me) * (0.25 * pull - 0.5 * sums[0:3])
+        if last:
+            line = scale[:, here] * field
+            out_ref[:, :, here] = jnp.broadcast_to(line[None], (out_ref.shape[0], 3, TILE))
+        else:
+            out_ref[:, here] = scale[:, here] * (state[3:6, here] + field)
+
+
+def centre_call(body, shapes, scratch, nb, arrays, after):
     size = arrays[0].shape[1]
-    shape = {"permanent": (6, size), "dipole": (3, size), "pulled": (copies, 3, size)}[mode]
     pairs = size * NBR * TILE
     return pl.pallas_call(
-        functools.partial(centre_kernel, mode, size // TILE),
-        out_shape=jax.ShapeDtypeStruct(shape, jnp.float32),
+        functools.partial(body, size // TILE),
+        out_shape=shapes,
         in_specs=[pl.BlockSpec(memory_space=SMEM)]
         + [pl.BlockSpec(memory_space=VMEM)] * len(arrays)
         + [pl.BlockSpec(memory_space=pl.ANY)] * len(after),
-        out_specs=pl.BlockSpec(memory_space=VMEM),
-        scratch_shapes=[
-            pltpu.VMEM((8, 3 * size), jnp.float32),
-            pltpu.VMEM((HALO_T, 3, TILE, TILE), jnp.float32),
-            pltpu.VMEM((HALO_T, 3, TILE, TILE), jnp.float32),
-        ],
+        out_specs=[pl.BlockSpec(memory_space=VMEM)] * len(shapes),
+        scratch_shapes=scratch,
         cost_estimate=pl.CostEstimate(
             flops=pairs * 100, bytes_accessed=4 * 24 * size, transcendentals=pairs
         ),
-        compiler_params=pltpu.CompilerParams(vmem_limit_bytes=16 << 20),
+        compiler_params=pltpu.CompilerParams(vmem_limit_bytes=12 << 20),
     )(nb, *arrays, *after)
+
+
+def centre_first(nb, after, *arrays):
+    size = arrays[0].shape[1]
+    shapes = [
+        jax.ShapeDtypeStruct((6, size), jnp.float32),
+        jax.ShapeDtypeStruct((size, NBR * TILE), jnp.bfloat16),
+        jax.ShapeDtypeStruct((size, NBR * TILE), jnp.bfloat16),
+    ]
+    scratch = [
+        pltpu.VMEM((8, 3 * size), jnp.float32),
+        pltpu.VMEM((48, 3 * size), jnp.bfloat16),
+        pltpu.VMEM((size, 48), jnp.bfloat16),
+        pltpu.VMEM((48, 3 * size), jnp.bfloat16),
+    ]
+    return centre_call(first_kernel, shapes, scratch, nb, arrays, after)
+
+
+def centre_next(copies, nb, after, *arrays):
+    size = arrays[0].shape[1]
+    shape = (copies, 3, size) if copies else (3, size)
+    scratch = [pltpu.VMEM((48, 3 * size), jnp.bfloat16)]
+    body = functools.partial(next_kernel, copies > 0)
+    shapes = [jax.ShapeDtypeStruct(shape, jnp.float32)]
+    return centre_call(body, shapes, scratch, nb, arrays, after)[0]
 
 
 def seat(order, odd, share):
@@ -368,30 +407,30 @@
 
     def fill(after):
         first = sum(plan[: len(short)])
-        short.append(short_range(ext8, neighbors, first, plan[len(short)], after))
+        short.append(short_range(ext8, neighbors.T, first, plan[len(short)], after))
         return short[-1]
 
     wait = fill(shares)
     cent, wait = lax.optimization_barrier((cent, wait))
     c3 = around(cent)
     wait = fill(cent)
-    state = centre("permanent", beads, (wait,), nb, *c3, near_charge, alpha)
+    state, *weights = centre_first(nb, (wait,), *c3, near_charge, alpha)
+
+    dip = state[:3]
+    for _ in range(ITERS):
+        d3 = around(dip)
+        dip = centre_next(0, nb, (fill(dip),), *c3, *d3, alpha, state, *weights)
+    d3 = around(dip)
+    pulled = centre_next(beads, nb, (fill(dip),), *c3, *d3, charge, state, *weights)
+    fill(pulled)
+    every = lax.all_to_all(pulled, "bead", 0, 0)
 
     turn = [(b, (b + 1) % beads) for b in range(beads)]
     turn_back = [(j, i) for i, j in turn]
-    late, state = lax.optimization_barrier((coords, state))
+    late, pulled = lax.optimization_barrier((coords, pulled))
     last = lax.ppermute(late, "bead", turn)
     following = lax.ppermute(late, "bead", turn_back)
-    dip = state[:3]
-    for sweep in range(ITERS):
-        d3 = around(dip)
-        hold = (fill(dip), last, following) if sweep == 1 else (fill(dip),)
-        dip = centre("dipole", beads, hold, nb, *c3, *d3, alpha, state)
-    d3 = around(dip)
     dipoles = lax.ppermute(dip, both, home)
-    pulled = centre("pulled", beads, (fill(dip), dipoles), nb, *c3, *d3, charge)
-    fill(pulled)
-    every = lax.all_to_all(pulled, "bead", 0, 0)
     forces, dipoles = total(
         order, plan, odd, coords, last, following, masses[None], every, dipoles, *short
     )

time: 110 us -> 97.2 us (0.88)
  the two profiles are of different devices: /device:TPU:6 before, /device:TPU:8 now
where the time goes in v3:
time: 97.2 us; the launch traced here: 96.8 us
  starting transfers between devices  47.8 us (49%)
  Pallas kernels  43.6 us (45%)
  local copies, waits for them, and re-layouts  3.46 us (4%)
    pallas_call x7, Pallas kernels, short_range(): pl.pallas_call(functools.partial(short_kernel, tiles, first), out_shape=j...  33.8 us
    all_to_all x1, starting transfers between devices, per_device(): every = lax.all_to_all(pulled, 'bead', 0, 0)  14.6 us
    all_to_all x1, starting transfers between devices, per_device(): cent = jnp.sum(lax.all_to_all(shares, 'bead', 0, 0), axis=0) / beads  11.8 us
    ppermute x10, starting transfers between devices, around(): return (lax.ppermute(x, both, fore), x, lax.ppermute(x, both, back))  11.7 us
    pallas_call x5, Pallas kernels, centre_call(): pl.pallas_call(functools.partial(body, size // TILE), out_shape=shapes, i...  8 us
    ppermute x1, starting transfers between devices, per_device(): after = lax.ppermute(first, 'space', down)  2.95 us
    ppermute x1, starting transfers between devices, per_device(): following = lax.ppermute(late, 'bead', turn_back)  2.67 us
    unnamed x13, local copies, waits for them, and re-layouts  2.54 us
  transfers between devices with their start and end apart: 17, of which 1 were waited for; matrix products, arithmetic and copies ran while one was open for 1% of the time, Pallas kernels for 35%

profile of v3, /device:TPU:8, one launch (start us, length us, event | category | flops | bytes accessed | tf_op | source)
XLA Modules:
  0.0 96.8 jit_solution(11128569597525384277)
XLA Ops:
  0.7 0.9 copy-done
  1.6 0.8 copy-done.2
  2.4 0.8 pack.1
  3.2 3.0 %collective-permute-start.1 = (f32[4,512]{1,0:T(4,128)S(1)}, f32[4,512]{1,0:T(4,128)S(1)}, u32[]{:S(2)}, u32[]{:S(2)}) collective-permute-start(f32[4,512]{1,0:T(4,128)S(1)} %get-tuple-element.14), channel_id=1, source_target_pairs={{1,0},{2,1},{3,2},{4,3},{5,4},{6,5},{7,6},{0,7},{9,8},{10,9},{11,1... | collective-permute-start | bytes 24584 | tf_op jit(solution)/shard_map/ppermute | solution.py:392
  6.1 11.8 %all-to-all-start = ((f32[32,3,512]{2,1,0:T(4,128)}), f32[32,3,512]{2,1,0:T(4,128)S(1)}, u32[]{:S(2)}, u32[]{:S(2)}) async-start(f32[32,3,512]{2,1,0:T(4,128)} %get-tuple-element.12.after_ref), calls=%async_computation | async-start | bytes 524288 | tf_op jit(solution)/shard_map/all_to_all | solution.py:397
  18.0 0.7 copy-done.5
  19.0 0.8 dynamic_slice.14
  19.9 8.3 %short_range.7.refs_0_ = f32[3,4608]{1,0:T(4,128)S(1)} custom-call(s32[8,128]{1,0:T(8,128)S(1)} %bitcast.21, f32[8,17408]{1,0:T(8,128)S(1)} %extend.1.ext_ref, f32[32,3,512]{2,1,0:T(4,128)} %get-tuple-element.12.after_ref), custom_call_target="tpu_custom_call" | custom-call | flops 471859200 | bytes 247808 | tf_op jit(solution)/shard_map/short_range/pallas_call | solution.py:119
  28.3 1.6 %collective-permute-start.2 = (f32[3,512]{1,0:T(4,128)S(1)}, f32[3,512]{1,0:T(4,128)S(1)}, u32[]{:S(2)}, u32[]{:S(2)}) collective-permute-start(f32[3,512]{1,0:T(4,128)S(1)} %broadcast_multiply_fusion.after_ref.own), channel_id=1, source_target_pairs={{0,8},{8,16},{16,24},{24,32},{32,40},{40,48},{48,56},{56,120},{120... | collective-permute-start | bytes 18440 | tf_op jit(solution)/shard_map/ppermute | solution.py:385
  30.4 4.4 %short_range.8.refs_0_.refs_1_ = f32[3,2048]{1,0:T(4,128)S(1)} custom-call(s32[8,128]{1,0:T(8,128)S(1)} %bitcast.22, f32[8,17408]{1,0:T(8,128)S(1)} %extend.1.ext_ref, f32[3,512]{1,0:T(4,128)S(1)} %broadcast_multiply_fusion.after_ref.own), custom_call_target="tpu_custom_call" | custom-call | flops 209715200 | bytes 135168 | tf_op jit(solution)/shard_map/short_range/pallas_call | solution.py:119
  34.9 1.7 %shard_map.68 = (f32[6,512]{1,0:T(8,128)S(1)}, bf16[512,1024]{1,0:T(8,128)(2,1)S(1)}, bf16[512,1024]{1,0:T(8,128)(2,1)S(1)}) custom-call(s32[4,8]{1,0:T(4,128)S(1)} %broadcast_subtract_fusion.nb_ref, f32[3,512]{1,0:T(4,128)S(1)} %collective-permute-done.2.before, f32[3,512]{1,0:T(4,128)S(1)} %broadcast_multiply_fusion.after_ref.own, ...), custom_call_target="tpu_custom_call" | custom-call | flops 52428800 | bytes 49152 | tf_op jit(solution)/shard_map/pallas_call | solution.py:226
  36.6 1.6 %collective-permute-start.4 = (f32[3,512]{1,0:T(4,128)S(1)}, f32[3,512]{1,0:T(4,128)S(1)}, u32[]{:S(2)}, u32[]{:S(2)}) collective-permute-start(f32[3,512]{1,0:T(4,128)S(1)} %slice.11.after_ref.dip_o), channel_id=1, source_target_pairs={{0,8},{8,16},{16,24},{24,32},{32,40},{40,48},{48,56},{56,120},{120... | collective-permute-start | bytes 18440 | tf_op jit(solution)/shard_map/ppermute | solution.py:385
  38.7 4.4 %short_range.9.refs_4_.refs_2_ = f32[3,2048]{1,0:T(4,128)S(1)} custom-call(s32[8,128]{1,0:T(8,128)S(1)} %bitcast.23, f32[8,17408]{1,0:T(8,128)S(1)} %extend.1.ext_ref, f32[3,512]{1,0:T(4,128)S(1)} %slice.11.after_ref.dip_o), custom_call_target="tpu_custom_call" | custom-call | flops 209715200 | bytes 135168 | tf_op jit(solution)/shard_map/short_range/pallas_call | solution.py:119
  43.2 1.4 %shard_map.69.after_ref.dip_o = f32[3,512]{1,0:T(4,128)S(1)} custom-call(s32[4,8]{1,0:T(4,128)S(1)} %broadcast_subtract_fusion.nb_ref, f32[3,512]{1,0:T(4,128)S(1)} %collective-permute-done.2.before, f32[3,512]{1,0:T(4,128)S(1)} %broadcast_multiply_fusion.after_ref.own, f32[3,512]{1,0:T(4,128)S(1)} %collective-permute-done.3.after, ...), custom_call_target="tpu_custom_call" | custom-call | flops 52428800 | bytes 49152 | tf_op jit(solution)/shard_map/pallas_call | solution.py:226
  44.6 1.5 %collective-permute-start.6 = (f32[3,512]{1,0:T(4,128)S(1)}, f32[3,512]{1,0:T(4,128)S(1)}, u32[]{:S(2)}, u32[]{:S(2)}) collective-permute-start(f32[3,512]{1,0:T(4,128)S(1)} %shard_map.69.after_ref.dip_o), channel_id=1, source_target_pairs={{0,8},{8,16},{16,24},{24,32},{32,40},{40,48},{48,56},{56,120},{120... | collective-permute-start | bytes 18440 | tf_op jit(solution)/shard_map/ppermute | solution.py:385
  46.1 0.6 collective-permute-start.7
  46.7 4.4 %short_range.10.refs_4_.refs_3_ = f32[3,2048]{1,0:T(4,128)S(1)} custom-call(s32[8,128]{1,0:T(8,128)S(1)} %bitcast.24, f32[8,17408]{1,0:T(8,128)S(1)} %extend.1.ext_ref, f32[3,512]{1,0:T(4,128)S(1)} %shard_map.69.after_ref.dip_o), custom_call_target="tpu_custom_call" | custom-call | flops 209715200 | bytes 135168 | tf_op jit(solution)/shard_map/short_range/pallas_call | solution.py:119
  51.1 1.4 %shard_map.70.after_ref.dip_o = f32[3,512]{1,0:T(4,128)S(1)} custom-call(s32[4,8]{1,0:T(4,128)S(1)} %broadcast_subtract_fusion.nb_ref, f32[3,512]{1,0:T(4,128)S(1)} %collective-permute-done.2.before, f32[3,512]{1,0:T(4,128)S(1)} %broadcast_multiply_fusion.after_ref.own, f32[3,512]{1,0:T(4,128)S(1)} %collective-permute-done.3.after, ...), custom_call_target="tpu_custom_call" | custom-call | flops 52428800 | bytes 49152 | tf_op jit(solution)/shard_map/pallas_call | solution.py:226
  52.5 1.5 %collective-permute-start.8 = (f32[3,512]{1,0:T(4,128)S(1)}, f32[3,512]{1,0:T(4,128)S(1)}, u32[]{:S(2)}, u32[]{:S(2)}) collective-permute-start(f32[3,512]{1,0:T(4,128)S(1)} %shard_map.70.after_ref.dip_o), channel_id=1, source_target_pairs={{0,8},{8,16},{16,24},{24,32},{32,40},{40,48},{48,56},{56,120},{120... | collective-permute-start | bytes 18440 | tf_op jit(solution)/shard_map/ppermute | solution.py:385
  54.6 4.4 %short_range.11.refs_4_ = f32[3,2048]{1,0:T(4,128)S(1)} custom-call(s32[8,128]{1,0:T(8,128)S(1)} %bitcast.25, f32[8,17408]{1,0:T(8,128)S(1)} %extend.1.ext_ref, f32[3,512]{1,0:T(4,128)S(1)} %shard_map.70.after_ref.dip_o), custom_call_target="tpu_custom_call" | custom-call | flops 209715200 | bytes 135168 | tf_op jit(solution)/shard_map/short_range/pallas_call | solution.py:119
  59.0 1.4 %shard_map.71.after_ref.dip_o = f32[3,512]{1,0:T(4,128)S(1)} custom-call(s32[4,8]{1,0:T(4,128)S(1)} %broadcast_subtract_fusion.nb_ref, f32[3,512]{1,0:T(4,128)S(1)} %collective-permute-done.2.before, f32[3,512]{1,0:T(4,128)S(1)} %broadcast_multiply_fusion.after_ref.own, f32[3,512]{1,0:T(4,128)S(1)} %collective-permute-done.3.after, ...), custom_call_target="tpu_custom_call" | custom-call | flops 52428800 | bytes 49152 | tf_op jit(solution)/shard_map/pallas_call | solution.py:226
  60.4 1.5 %collective-permute-start.10 = (f32[3,512]{1,0:T(4,128)S(1)}, f32[3,512]{1,0:T(4,128)S(1)}, u32[]{:S(2)}, u32[]{:S(2)}) collective-permute-start(f32[3,512]{1,0:T(4,128)S(1)} %shard_map.71.after_ref.dip_o), channel_id=1, source_target_pairs={{0,8},{8,16},{16,24},{24,32},{32,40},{40,48},{48,56},{56,120},{120... | collective-permute-start | bytes 18440 | tf_op jit(solution)/shard_map/ppermute | solution.py:385
  62.0 1.7 %collective-permute-start.11 = (f32[3,512]{1,0:T(4,128)S(1)}, f32[3,512]{1,0:T(4,128)S(1)}, u32[]{:S(2)}, u32[]{:S(2)}) collective-permute-start(f32[3,512]{1,0:T(4,128)S(1)} %shard_map.71.after_ref.dip_o), channel_id=1, source_target_pairs={{8,0},{16,8},{24,16},{32,24},{40,32},{48,40},{56,48},{120,56},{112... | collective-permute-start | bytes 18440 | tf_op jit(solution)/shard_map/ppermute | solution.py:385
  63.7 4.4 %short_range.12.refs_4_.refs_5_ = f32[3,2048]{1,0:T(4,128)S(1)} custom-call(s32[8,128]{1,0:T(8,128)S(1)} %bitcast.26, f32[8,17408]{1,0:T(8,128)S(1)} %extend.1.ext_ref, f32[3,512]{1,0:T(4,128)S(1)} %shard_map.71.after_ref.dip_o), custom_call_target="tpu_custom_call" | custom-call | flops 209715200 | bytes 135168 | tf_op jit(solution)/shard_map/short_range/pallas_call | solution.py:119
  68.2 2.1 %shard_map.72.after_ref = f32[32,3,512]{2,1,0:T(4,128)} custom-call(s32[4,8]{1,0:T(4,128)S(1)} %broadcast_subtract_fusion.nb_ref, f32[3,512]{1,0:T(4,128)S(1)} %collective-permute-done.2.before, f32[3,512]{1,0:T(4,128)S(1)} %broadcast_multiply_fusion.after_ref.own, f32[3,512]{1,0:T(4,128)S(1)} %collective-permute-done.3.after, ...), custom_call_target="tpu_custom_call" | custom-call | flops 52428800 | bytes 49152 | tf_op jit(solution)/shard_map/pallas_call | solution.py:226
  70.3 14.6 %all-to-all-start.1 = ((f32[32,3,512]{2,1,0:T(4,128)}), f32[32,3,512]{2,1,0:T(4,128)S(1)}, u32[]{:S(2)}, u32[]{:S(2)}) async-start(f32[32,3,512]{2,1,0:T(4,128)} %shard_map.72.after_ref), calls=%async_computation.1 | async-start | bytes 524288 | tf_op jit(solution)/shard_map/all_to_all | solution.py:426
  84.9 1.5 %collective-permute-start.12 = (f32[3,1,16384]{2,1,0:T(1,128)S(1)}, f32[3,1,16384]{2,1,0:T(1,128)S(1)}, u32[]{:S(2)}, u32[]{:S(2)}) collective-permute-start(f32[3,1,16384]{2,1,0:T(1,128)S(1)} %bitcast.10), channel_id=1, source_target_pairs={{0,8},{8,16},{16,24},{24,32},{32,40},{40,48},{48,56},{56,64},{64,7... | collective-permute-start | bytes 589832 | tf_op jit(solution)/shard_map/ppermute | solution.py:431
  86.5 2.7 %collective-permute-start.13 = (f32[3,1,16384]{2,1,0:T(1,128)S(1)}, f32[3,1,16384]{2,1,0:T(1,128)S(1)}, u32[]{:S(2)}, u32[]{:S(2)}) collective-permute-start(f32[3,1,16384]{2,1,0:T(1,128)S(1)} %bitcast.11), channel_id=1, source_target_pairs={{8,0},{16,8},{24,16},{32,24},{40,32},{48,40},{56,48},{64,56},{72,6... | collective-permute-start | bytes 589832 | tf_op jit(solution)/shard_map/ppermute | solution.py:432
  89.1 2.5 %collective-permute-start.14 = (f32[3,512]{1,0:T(4,128)S(1)}, f32[3,512]{1,0:T(4,128)S(1)}, u32[]{:S(2)}, u32[]{:S(2)}) collective-permute-start(f32[3,512]{1,0:T(4,128)S(1)} %shard_map.71.after_ref.dip_o), channel_id=1, source_target_pairs={{0,0},{8,8},{16,16},{24,24},{32,32},{40,40},{48,48},{56,56},{120,6... | collective-permute-start | bytes 18440 | tf_op jit(solution)/shard_map/ppermute | solution.py:433
  91.6 3.5 %short_range.13.refs_6_ = f32[3,1536]{1,0:T(4,128)S(1)} custom-call(s32[8,128]{1,0:T(8,128)S(1)} %bitcast.27, f32[8,17408]{1,0:T(8,128)S(1)} %extend.1.ext_ref, f32[32,3,512]{2,1,0:T(4,128)} %shard_map.72.after_ref), custom_call_target="tpu_custom_call" | custom-call | flops 157286400 | bytes 112640 | tf_op jit(solution)/shard_map/short_range/pallas_call | solution.py:119
  95.1 0.8 collective-permute-done.14.dip
  95.9 0.9 total.1
  (40 shorter events, 2.2 us)
Async XLA Ops:
  0.6 0.9 copy-start
  1.6 0.8 copy-start.2
  3.2 16.6 %collective-permute-start = (f32[4,512]{1,0:T(4,128)S(1)}, f32[4,512]{1,0:T(4,128)S(1)}, u32[]{:S(2)}, u32[]{:S(2)}) collective-permute-start(f32[4,512]{1,0:T(4,128)S(1)} %get-tuple-element.13), channel_id=1, source_target_pairs={{0,1},{1,2},{2,3},{3,4},{4,5},{5,6},{6,7},{7,0},{8,9},{9,10},{10,1... | collective-permute-start | bytes 24584 | tf_op jit(solution)/shard_map/ppermute | solution.py:391
  3.2 16.6 %collective-permute-start.1 = (f32[4,512]{1,0:T(4,128)S(1)}, f32[4,512]{1,0:T(4,128)S(1)}, u32[]{:S(2)}, u32[]{:S(2)}) collective-permute-start(f32[4,512]{1,0:T(4,128)S(1)} %get-tuple-element.14), channel_id=1, source_target_pairs={{1,0},{2,1},{3,2},{4,3},{5,4},{6,5},{7,6},{0,7},{9,8},{10,9},{11,1... | collective-permute-start | bytes 24584 | tf_op jit(solution)/shard_map/ppermute | solution.py:392
  6.1 13.6 %copy-start.1 = (f32[1,3,16384]{2,0,1:T(1,128)S(1)}, f32[1,3,16384]{2,0,1:T(1,128)}, u32[]{:S(2)}) copy-start(f32[1,3,16384]{2,0,1:T(1,128)} %param.5) | copy-start | bytes 589828
  6.1 22.1 %all-to-all-start = ((f32[32,3,512]{2,1,0:T(4,128)}), f32[32,3,512]{2,1,0:T(4,128)S(1)}, u32[]{:S(2)}, u32[]{:S(2)}) async-start(f32[32,3,512]{2,1,0:T(4,128)} %get-tuple-element.12.after_ref), calls=%async_computation | async-start | bytes 524288 | tf_op jit(solution)/shard_map/all_to_all | solution.py:397
  18.0 0.9 copy-start.3
  18.0 0.7 copy-start.5
  28.3 6.5 %collective-permute-start.2 = (f32[3,512]{1,0:T(4,128)S(1)}, f32[3,512]{1,0:T(4,128)S(1)}, u32[]{:S(2)}, u32[]{:S(2)}) collective-permute-start(f32[3,512]{1,0:T(4,128)S(1)} %broadcast_multiply_fusion.after_ref.own), channel_id=1, source_target_pairs={{0,8},{8,16},{16,24},{24,32},{32,40},{40,48},{48,56},{56,120},{120... | collective-permute-start | bytes 18440 | tf_op jit(solution)/shard_map/ppermute | solution.py:385
  29.9 5.0 %collective-permute-start.3 = (f32[3,512]{1,0:T(4,128)S(1)}, f32[3,512]{1,0:T(4,128)S(1)}, u32[]{:S(2)}, u32[]{:S(2)}) collective-permute-start(f32[3,512]{1,0:T(4,128)S(1)} %broadcast_multiply_fusion.after_ref.own), channel_id=1, source_target_pairs={{8,0},{16,8},{24,16},{32,24},{40,32},{48,40},{56,48},{120,56},{112... | collective-permute-start | bytes 18440 | tf_op jit(solution)/shard_map/ppermute | solution.py:385
  36.6 6.5 %collective-permute-start.4 = (f32[3,512]{1,0:T(4,128)S(1)}, f32[3,512]{1,0:T(4,128)S(1)}, u32[]{:S(2)}, u32[]{:S(2)}) collective-permute-start(f32[3,512]{1,0:T(4,128)S(1)} %slice.11.after_ref.dip_o), channel_id=1, source_target_pairs={{0,8},{8,16},{16,24},{24,32},{32,40},{40,48},{48,56},{56,120},{120... | collective-permute-start | bytes 18440 | tf_op jit(solution)/shard_map/ppermute | solution.py:385
  38.2 5.0 %collective-permute-start.5 = (f32[3,512]{1,0:T(4,128)S(1)}, f32[3,512]{1,0:T(4,128)S(1)}, u32[]{:S(2)}, u32[]{:S(2)}) collective-permute-start(f32[3,512]{1,0:T(4,128)S(1)} %slice.11.after_ref.dip_o), channel_id=1, source_target_pairs={{8,0},{16,8},{24,16},{32,24},{40,32},{48,40},{56,48},{120,56},{112... | collective-permute-start | bytes 18440 | tf_op jit(solution)/shard_map/ppermute | solution.py:385
  44.6 6.5 %collective-permute-start.6 = (f32[3,512]{1,0:T(4,128)S(1)}, f32[3,512]{1,0:T(4,128)S(1)}, u32[]{:S(2)}, u32[]{:S(2)}) collective-permute-start(f32[3,512]{1,0:T(4,128)S(1)} %shard_map.69.after_ref.dip_o), channel_id=1, source_target_pairs={{0,8},{8,16},{16,24},{24,32},{32,40},{40,48},{48,56},{56,120},{120... | collective-permute-start | bytes 18440 | tf_op jit(solution)/shard_map/ppermute | solution.py:385
  46.1 5.0 %collective-permute-start.7 = (f32[3,512]{1,0:T(4,128)S(1)}, f32[3,512]{1,0:T(4,128)S(1)}, u32[]{:S(2)}, u32[]{:S(2)}) collective-permute-start(f32[3,512]{1,0:T(4,128)S(1)} %shard_map.69.after_ref.dip_o), channel_id=1, source_target_pairs={{8,0},{16,8},{24,16},{32,24},{40,32},{48,40},{56,48},{120,56},{112... | collective-permute-start | bytes 18440 | tf_op jit(solution)/shard_map/ppermute | solution.py:385
  52.5 6.5 %collective-permute-start.8 = (f32[3,512]{1,0:T(4,128)S(1)}, f32[3,512]{1,0:T(4,128)S(1)}, u32[]{:S(2)}, u32[]{:S(2)}) collective-permute-start(f32[3,512]{1,0:T(4,128)S(1)} %shard_map.70.after_ref.dip_o), channel_id=1, source_target_pairs={{0,8},{8,16},{16,24},{24,32},{32,40},{40,48},{48,56},{56,120},{120... | collective-permute-start | bytes 18440 | tf_op jit(solution)/shard_map/ppermute | solution.py:385
  54.0 5.0 %collective-permute-start.9 = (f32[3,512]{1,0:T(4,128)S(1)}, f32[3,512]{1,0:T(4,128)S(1)}, u32[]{:S(2)}, u32[]{:S(2)}) collective-permute-start(f32[3,512]{1,0:T(4,128)S(1)} %shard_map.70.after_ref.dip_o), channel_id=1, source_target_pairs={{8,0},{16,8},{24,16},{32,24},{40,32},{48,40},{56,48},{120,56},{112... | collective-permute-start | bytes 18440 | tf_op jit(solution)/shard_map/ppermute | solution.py:385
  60.4 7.7 %collective-permute-start.10 = (f32[3,512]{1,0:T(4,128)S(1)}, f32[3,512]{1,0:T(4,128)S(1)}, u32[]{:S(2)}, u32[]{:S(2)}) collective-permute-start(f32[3,512]{1,0:T(4,128)S(1)} %shard_map.71.after_ref.dip_o), channel_id=1, source_target_pairs={{0,8},{8,16},{16,24},{24,32},{32,40},{40,48},{48,56},{56,120},{120... | collective-permute-start | bytes 18440 | tf_op jit(solution)/shard_map/ppermute | solution.py:385
  62.0 6.2 %collective-permute-start.11 = (f32[3,512]{1,0:T(4,128)S(1)}, f32[3,512]{1,0:T(4,128)S(1)}, u32[]{:S(2)}, u32[]{:S(2)}) collective-permute-start(f32[3,512]{1,0:T(4,128)S(1)} %shard_map.71.after_ref.dip_o), channel_id=1, source_target_pairs={{8,0},{16,8},{24,16},{32,24},{40,32},{48,40},{56,48},{120,56},{112... | collective-permute-start | bytes 18440 | tf_op jit(solution)/shard_map/ppermute | solution.py:385
  70.3 25.6 %all-to-all-start.1 = ((f32[32,3,512]{2,1,0:T(4,128)}), f32[32,3,512]{2,1,0:T(4,128)S(1)}, u32[]{:S(2)}, u32[]{:S(2)}) async-start(f32[32,3,512]{2,1,0:T(4,128)} %shard_map.72.after_ref), calls=%async_computation.1 | async-start | bytes 524288 | tf_op jit(solution)/shard_map/all_to_all | solution.py:426
  84.9 11.0 %copy-start.4 = (f32[16384]{0:T(1024)S(1)}, f32[16384]{0:T(1024)}, u32[]{:S(2)}) copy-start(f32[16384]{0:T(1024)} %param.8) | copy-start | bytes 196612
  84.9 11.0 %collective-permute-start.12 = (f32[3,1,16384]{2,1,0:T(1,128)S(1)}, f32[3,1,16384]{2,1,0:T(1,128)S(1)}, u32[]{:S(2)}, u32[]{:S(2)}) collective-permute-start(f32[3,1,16384]{2,1,0:T(1,128)S(1)} %bitcast.10), channel_id=1, source_target_pairs={{0,8},{8,16},{16,24},{24,32},{32,40},{40,48},{48,56},{56,64},{64,7... | collective-permute-start | bytes 589832 | tf_op jit(solution)/shard_map/ppermute | solution.py:431
  86.5 9.4 %collective-permute-start.13 = (f32[3,1,16384]{2,1,0:T(1,128)S(1)}, f32[3,1,16384]{2,1,0:T(1,128)S(1)}, u32[]{:S(2)}, u32[]{:S(2)}) collective-permute-start(f32[3,1,16384]{2,1,0:T(1,128)S(1)} %bitcast.11), channel_id=1, source_target_pairs={{8,0},{16,8},{24,16},{32,24},{40,32},{48,40},{56,48},{64,56},{72,6... | collective-permute-start | bytes 589832 | tf_op jit(solution)/shard_map/ppermute | solution.py:432
  89.1 6.7 %collective-permute-start.14 = (f32[3,512]{1,0:T(4,128)S(1)}, f32[3,512]{1,0:T(4,128)S(1)}, u32[]{:S(2)}, u32[]{:S(2)}) collective-permute-start(f32[3,512]{1,0:T(4,128)S(1)} %shard_map.71.after_ref.dip_o), channel_id=1, source_target_pairs={{0,0},{8,8},{16,16},{24,24},{32,32},{40,40},{48,48},{56,56},{120,6... | collective-permute-start | bytes 18440 | tf_op jit(solution)/shard_map/ppermute | solution.py:433
